TPU v7x, 128 devices: a whole 4x4x4 slice. The times are simulated.
128 devices in a mesh: grp: 8 (over z, core), blk: 16 (over x, y).
Axes of the slice: x: 4, y: 4, z: 4, core: 2. Of those that a mesh axis runs over, the one named last changes fastest.
Arguments:
- chol_done: float32 [622592, 512], P(('grp', 'blk')), as said below
- new_cols: float32 [622592, 384], P(('grp', 'blk')), as said below
- diag_entries: float32 [622592], P(('grp', 'blk')), as said below
- pivots: int32 [2, 192], replicated, may hold values from 0 to 622591, as said below
- live_blocks: int32 [128], replicated, may hold values from 1 to 19, as said below
Outputs:
- new_vectors: float32 [622592, 384], P(('grp', 'blk'))
- left_ratio: float32 [1], replicated
Inputs may be any that keep to these rules, and one draw needn't show every extreme that they name: The pivots of both panels are 384 distinct pair rows, all screened in; each device's rows hold at most 3 pivots of one panel, and some device holds exactly 3 in each panel. `live_blocks`: some device has all its blocks screened in; the screened-in blocks of a device come first. `chol_done`: rows of screened-out blocks are zero. `new_cols`: rows of screened-out blocks are zero; each panel's block at its pivot rows, after all earlier vectors are subtracted, is symmetric positive definite. `diag_entries`: entries of screened-out rows are zero.
All inputs are finite; a program needn't handle non-finite values.
Results may differ from a plain program's by a relative error of at most 0.00011.
Values sent between devices are 32-bit elements; how exact they have to be, the bound alone decides.
A program may use at most 128 MiB of HBM per device.

v0:
```python
import jax
import jax.numpy as jnp
from jax import lax
from jax.sharding import PartitionSpec as P

BLOCK_ROWS = 256


def factor_inverse(head_cols, heads):
    block = head_cols
    for head in heads:
        block = block - jnp.dot(head, head.T, precision=lax.Precision.HIGHEST)
    lower = jnp.linalg.cholesky(block)
    return lax.linalg.triangular_solve(
        lower, jnp.eye(block.shape[0], dtype=jnp.float32), left_side=True, lower=True
    )


def body(chol_done, new_cols, diag_entries, pivots, live_blocks):
    rows = chol_done.shape[0]
    order = new_cols.shape[1] // 2
    me = lax.axis_index(("grp", "blk"))
    live_count = lax.dynamic_index_in_dim(live_blocks, me, keepdims=False)
    mask = (jnp.arange(rows) < live_count * BLOCK_ROWS).astype(jnp.float32)

    def collect(arrays, wanted):
        owner = wanted // rows
        local = wanted - owner * rows
        mine = owner == me
        safe = jnp.where(mine, local, 0)
        parts = tuple((jnp.where(mine[:, None], source[safe], 0.0) for source in arrays))
        return lax.psum(parts, ("grp", "blk"))

    def local_panel(cols, factors, heads, inverse):
        resid = cols
        for factor, head in zip(factors, heads):
            resid = resid - jnp.dot(factor, head.T, precision=lax.Precision.HIGHEST)
        return jnp.dot(resid * mask[:, None], inverse.T, precision=lax.Precision.HIGHEST)

    cols_first = new_cols[:, :order]
    cols_second = new_cols[:, order:]
    done_head, cols_head = collect((chol_done, cols_first), pivots[0])
    inverse_first = factor_inverse(cols_head, (done_head,))
    first = local_panel(cols_first, (chol_done,), (done_head,), inverse_first)
    done_next, first_next, cols_next = collect((chol_done, first, cols_second), pivots[1])
    inverse_second = factor_inverse(cols_next, (done_next, first_next))
    second = local_panel(cols_second, (chol_done, first), (done_next, first_next), inverse_second)
    left = diag_entries - jnp.sum(chol_done * chol_done, axis=1)
    left = left - jnp.sum(first * first, axis=1)
    left = (left - jnp.sum(second * second, axis=1)) * mask
    top_left, top_diag = lax.pmax((jnp.max(left), jnp.max(diag_entries * mask)), ("grp", "blk"))
    ratio = top_left / top_diag
    return (jnp.concatenate([first, second], axis=1), ratio.reshape(1))


def solution(mesh):
    placed = (P(("grp", "blk"), None), P(("grp", "blk"), None), P(("grp", "blk")), P(), P())
    return jax.shard_map(
        body, mesh=mesh, in_specs=placed, out_specs=(P(("grp", "blk"), None), P()), check_vma=False
    )
```

profile of v0, /device:TPU:0, one launch (start us, length us, event | category | flops | bytes accessed | tf_op | source)
XLA Modules:
  0.0 582.3 jit_solution(4591455716951936747)
XLA Ops:
  7.2 0.8 and_reduce_fusion.1
  8.0 0.8 broadcast_divide_fusion.1
  8.8 0.8 compare_select_fusion.1
  9.6 9.1 %fusion.36 = (f32[4864,192]{1,0:T(8,128)}, f32[4864,192]{1,0:T(8,128)}) fusion(f32[4864,384]{1,0:T(8,128)} %param.9), kind=kLoop, calls=%fused_computation.119 | loop fusion | bytes 14942208 | tf_op jit(solution)/shard_map/slice | solution.py:41
  18.7 4.9 gather_fusion
  23.6 3.3 gather_fusion.1
  27.0 0.8 broadcast_select_fusion.1
  27.9 0.7 broadcast_select_fusion.4
  28.7 0.6 dynamic_slice.4
  30.0 4.9 gather_fusion.2
  34.9 3.3 gather_fusion.4
  38.3 0.8 broadcast_select_fusion
  39.1 139.5 %all-reduce.11.cloned.1.call-done = (f32[192,512]{1,0:T(8,128)}, f32[192,192]{0,1:T(8,128)}) async-done(((f32[192,512]{1,0:T(8,128)}, f32[192,192]{0,1:T(8,128)}), (f32[192,512]{1,0:T(8,128)}, f32[192,192]{0,1:T(8,128)})) %all-reduce.11.cloned.1.call-update) | async-done | bytes 540688 | tf_op jit(solution)/shard_map/psum | solution.py:32
  178.6 1.7 convolution_subtract_fusion.3
  180.5 11.7 %cholesky.136 = f32[128,128]{1,0:T(8,128)S(1)} custom-call(f32[128,128]{1,0:T(8,128)S(1)} %cholesky.208), custom_call_target="Cholesky" | custom-call | tf_op jit(solution)/shard_map/jit(cholesky)/cholesky | solution.py:13
  192.2 0.6 compare_reduce_fusion.3
  192.9 9.8 %custom-call.13 = f32[1,128,128]{1,2,0:T(8,128)S(1)} custom-call(f32[1,128,128]{2,1,0:T(8,128)S(1)} %get-tuple-element.50), custom_call_target="InvertDiagBlocksLowerTriangular" | custom-call | tf_op jit(solution)/shard_map/jit(cholesky)/cholesky | solution.py:13
  203.1 5.8 %cholesky.156 = f32[64,64]{1,0:T(8,128)S(1)} custom-call(f32[64,64]{1,0:T(8,128)S(1)} %convolution_subtract_fusion.7), custom_call_target="Cholesky" | custom-call | tf_op jit(solution)/shard_map/jit(cholesky)/cholesky | solution.py:13
  209.0 0.7 compare_reduce_fusion.2
  211.1 19.8 %custom-call.14 = f32[2,128,128]{1,2,0:T(8,128)S(1)} custom-call(f32[2,128,128]{2,1,0:T(8,128)S(1)} %pad_maximum_fusion.1), custom_call_target="InvertDiagBlocksLowerTriangular" | custom-call | tf_op jit(solution)/shard_map/triangular_solve/custom-call.0 | solution.py:14
  230.9 0.4 fusion.17
  231.3 0.3 convolution_subtract_fusion.5
  231.6 0.3 fusion.29
  232.0 13.0 %fusion.3 = f32[4864,192]{1,0:T(8,128)S(1)} fusion(f32[192,512]{1,0:T(8,128)S(1)} %copy-done.1, f32[4864,512]{1,0:T(8,128)} %param.8, f32[4864]{0:T(1024)S(1)} %fusion.31, f32[4864,384]{1,0:T(8,128)} %param.9), kind=kOutput, calls=%fused_computation.13 | convolution fusion | flops 5739675648 | bytes 17845248 | tf_op jit(solution)/shard_map/dot_general | solution.py:37
  245.0 7.3 %multiply_reduce_fusion.2 = (f32[4864]{0:T(1024)S(1)}, f32[4864,192]{0,1:T(8,128)}) fusion(f32[4864,192]{1,0:T(8,128)S(1)} %fusion.3, f32[64,192]{0,1:T(8,128)S(1)} %fusion.29, f32[128,192]{0,1:T(8,128)S(1)} %fusion.17), kind=kOutput, calls=%fused_computation.15 | convolution fusion | flops 2153577728 | bytes 7638016 | tf_op jit(solution)/shard_map/dot_general | solution.py:38
  252.3 5.8 copy.20
  258.1 3.3 gather_fusion.3
  261.5 0.8 broadcast_select_fusion.2
  262.3 4.6 multiply_reduce_fusion
  266.9 142.3 %all-reduce.9.cloned.1.call-done = (f32[192,512]{1,0:T(8,128)}, f32[192,192]{0,1:T(8,128)}, f32[192,192]{0,1:T(8,128)}) async-done(((f32[192,512]{1,0:T(8,128)}, f32[192,192]{0,1:T(8,128)}, f32[192,192]{0,1:T(8,128)}), (f32[192,512]{1,0:T(8,128)}, f32[192,192]{0,1:T(8,128)}, f32[192,192]{0,1:T(8,128)})) %all-reduce.9.cloned.1.call-update) | async-done | bytes 688144 | tf_op jit(solution)/shard_map/psum | solution.py:32
  409.1 1.7 convolution_subtract_fusion.2
  410.8 1.6 convolution_subtract_fusion.1
  412.6 11.7 %cholesky.174 = f32[128,128]{1,0:T(8,128)S(1)} custom-call(f32[128,128]{1,0:T(8,128)S(1)} %cholesky.211), custom_call_target="Cholesky" | custom-call | tf_op jit(solution)/shard_map/jit(cholesky)/cholesky | solution.py:13
  424.4 0.6 compare_reduce_fusion.1
  425.0 9.8 %custom-call.15 = f32[1,128,128]{1,2,0:T(8,128)S(1)} custom-call(f32[1,128,128]{2,1,0:T(8,128)S(1)} %get-tuple-element.48), custom_call_target="InvertDiagBlocksLowerTriangular" | custom-call | tf_op jit(solution)/shard_map/jit(cholesky)/cholesky | solution.py:13
  435.2 5.8 %cholesky.194 = f32[64,64]{1,0:T(8,128)S(1)} custom-call(f32[64,64]{1,0:T(8,128)S(1)} %convolution_subtract_fusion.6), custom_call_target="Cholesky" | custom-call | tf_op jit(solution)/shard_map/jit(cholesky)/cholesky | solution.py:13
  441.1 0.7 compare_reduce_fusion
  443.1 13.7 %fusion.1 = f32[4864,192]{1,0:T(8,128)} fusion(f32[192,512]{1,0:T(8,128)} %get-tuple-element.38, f32[4864,512]{1,0:T(8,128)} %param.8, f32[4864,384]{1,0:T(8,128)} %param.9), kind=kOutput, calls=%fused_computation.10 | convolution fusion | flops 5738741760 | bytes 17825792 | tf_op jit(solution)/shard_map/dot_general | solution.py:37
  456.9 19.8 %custom-call.16 = f32[2,128,128]{1,2,0:T(8,128)S(1)} custom-call(f32[2,128,128]{2,1,0:T(8,128)S(1)} %pad_maximum_fusion.2), custom_call_target="InvertDiagBlocksLowerTriangular" | custom-call | tf_op jit(solution)/shard_map/triangular_solve/custom-call.0 | solution.py:14
  476.8 0.4 fusion.15
  477.1 0.3 convolution_subtract_fusion.4
  477.5 0.3 fusion.26
  477.8 12.8 %fusion = f32[4864,192]{1,0:T(8,128)S(1)} fusion(f32[4864,192]{1,0:T(8,128)} %fusion.1, f32[4864,192]{0,1:T(8,128)} %get-tuple-element.68, f32[192,192]{0,1:T(8,128)S(1)} %copy-done.2, f32[4864]{0:T(1024)S(1)} %fusion.31), kind=kOutput, calls=%fused_computation.8 | convolution fusion | flops 2153545728 | bytes 11373568 | tf_op jit(solution)/shard_map/dot_general | solution.py:37
  490.7 5.8 %multiply_reduce_fusion.1 = (f32[4864]{0:T(1024)S(1)}, f32[4864,192]{0,1:T(8,128)S(1)}) fusion(f32[4864,192]{1,0:T(8,128)S(1)} %fusion, f32[64,192]{0,1:T(8,128)S(1)} %fusion.26, f32[128,192]{0,1:T(8,128)S(1)} %fusion.15), kind=kOutput, calls=%fused_computation.14 | convolution fusion | flops 2153577728 | bytes 7638016 | tf_op jit(solution)/shard_map/dot_general | solution.py:38
  496.5 3.5 pad_maximum_fusion
  500.0 8.6 %copy.26 = f32[4864,384]{1,0:T(8,128)} copy(f32[4864,384]{0,1:T(8,128)} %pad_maximum_fusion) | data formatting | bytes 14942208
  508.5 0.7 select_reduce_fusion.4
  509.2 63.6 %all-reduce.5 = (f32[]{:T(128)}, f32[]{:T(128)}) all-reduce(f32[]{:T(128)} %get-tuple-element.35, f32[]{:T(128)} %get-tuple-element.34), channel_id=1, replica_groups=mesh['grp'=8,'blk'=16] {'grp','blk'}, use_global_device_ids=true, to_apply=%region_13.16 | all-reduce | flops 2 | bytes 16 | tf_op jit(solution)/shard_map/pmax | solution.py:51
  (50 shorter events, 2.0 us)
Async XLA Ops:
  7.2 171.4 %all-reduce.11.cloned.1.call-start = ((), (), s32[]{:S(2)}) async-start(), calls=%async_computation.1 | async-start | bytes 1179648 | tf_op jit(solution)/shard_map/psum | solution.py:32
  18.7 9.9 %copy-start.4 = (s32[128]{0:T(128)S(1)}, s32[128]{0:T(128)}, u32[]{:S(2)}) copy-start(s32[128]{0:T(128)} %param.12) | copy-start | bytes 1540
  28.6 380.6 %all-reduce.9.cloned.1.call-start = ((), (), s32[]{:S(2)}) async-start(), calls=%async_computation | async-start | bytes 1572864 | tf_op jit(solution)/shard_map/psum | solution.py:32
  178.6 53.4 %copy-start.1 = (f32[192,512]{1,0:T(8,128)S(1)}, f32[192,512]{1,0:T(8,128)}, u32[]{:S(2)}) copy-start(f32[192,512]{1,0:T(8,128)} %get-tuple-element.41) | copy-start | bytes 1179652
  443.1 34.7 %copy-start.2 = (f32[192,192]{0,1:T(8,128)S(1)}, f32[192,192]{0,1:T(8,128)}, u32[]{:S(2)}) copy-start(f32[192,192]{0,1:T(8,128)} %get-tuple-element.39) | copy-start | bytes 442372
  490.6 5.8 %copy-start = (f32[4864,192]{0,1:T(8,128)S(1)}, f32[4864,192]{0,1:T(8,128)}, u32[]{:S(2)}) copy-start(f32[4864,192]{0,1:T(8,128)} %get-tuple-element.68) | copy-start | bytes 11206660
  500.0 8.6 %copy-start.3 = (f32[4864]{0:T(1024)S(1)}, f32[4864]{0:T(1024)}, u32[]{:S(2)}) copy-start(f32[4864]{0:T(1024)} %param.10) | copy-start | bytes 58372
Sparse Core Ops, SparseCore 0:
  28.7 149.8 all-reduce.10
  262.4 146.6 all-reduce.8
where the time goes:
time: 592 us; the launch traced here: 582 us
  waiting for transfers between devices  282 us (48%)
  other arithmetic  112 us (19%)
  blocking collectives  63.6 us (11%)
  matrix products  60.4 us (10%)
  local copies, waits for them, and re-layouts  44.3 us (7%)
  between operations  20.4 us (3%)
    psum x2, waiting for transfers between devices, collect(): return lax.psum(parts, ('grp', 'blk'))  282 us
    pmax x1, blocking collectives, body(): lax.pmax((jnp.max(left), jnp.max(diag_entries * mask)), ('grp', 'blk'))  63.6 us
    another operation x14, other arithmetic, factor_inverse(): lower = jnp.linalg.cholesky(block)  57.5 us
    another operation x10, other arithmetic, factor_inverse(): lax.linalg.triangular_solve(lower, jnp.eye(block.shape[0], dtype=jnp.floa...  39.9 us
    dot_general x3, matrix products, local_panel(): resid = resid - jnp.dot(factor, head.T, precision=lax.Precision.HIGHEST)  39.5 us
    gather x8, local copies, waits for them, and re-layouts, collect(): source[safe]  19.9 us
    dot_general x2, matrix products, local_panel(): jnp.dot(resid * mask[:, None], inverse.T, precision=lax.Precision.HIGHEST)  13.1 us
  transfers between devices with their start and end apart: 2, of which 2 were waited for; matrix products, arithmetic and copies ran while one was open for 2% of the time, Pallas kernels for 0%

commit v1 on v0

v1 whole, which is shorter than its diff:
```python
import jax
import jax.numpy as jnp
from jax import lax
from jax.experimental import pallas as pl
from jax.experimental.pallas import tpu as pltpu
from jax.sharding import PartitionSpec as P

MESH = pl.DeviceIdType.MESH
HIGHEST = lax.Precision.HIGHEST
F32 = jnp.float32
BF16 = jnp.bfloat16
ROWS = 4864
K = 512
ORDER = 192
COLS = 384
BLOCK_ROWS = 256
SLOTS = 3
SLOT_ROWS = 40
STEP = 16
ROUNDS = ORDER // STEP
TILE = 384
LAST = ROWS - ROUNDS * TILE
CHUNKS = [(i * TILE, TILE) for i in range(ROUNDS)] + [(ROUNDS * TILE, LAST)]
VMEM_LIMIT = 60 * 1024 * 1024
COLOURS = ((0, 16, "yxz"), (16, 16, "xzy"), (32, 8, "zyx"))


def slot_base(panel, slot):
    return slot * 6 if panel == 0 else 18 + slot * 7


def pick_kernel(piv_ref, chol_hbm, cols_hbm, out_ref, cbuf, nbuf, sem):
    me = lax.axis_index("grp") * 16 + lax.axis_index("blk")
    base = me * ROWS
    local = piv_ref[...] - base
    mine = (local >= 0) & (local < ROWS)
    spot = lax.broadcasted_iota(jnp.int32, (2, ORDER), 1)
    key = jnp.where(mine, (spot * 8192 + local).astype(F32), 4.0e6)
    found = []
    for slot in range(SLOTS):
        least = jnp.min(key, axis=1, keepdims=True)
        found.append(least)
        key = jnp.where(key <= least, 4.0e6, key)
    copies = []
    where_row = []
    for panel in range(2):
        for slot in range(SLOTS):
            value = found[slot][panel, 0].astype(jnp.int32)
            row = jnp.where(value < 4000000, value & 8191, 0)
            row = jnp.minimum(row, ROWS - 1)
            group = pl.multiple_of((row // 8) * 8, 8)
            n = panel * SLOTS + slot
            one = pltpu.make_async_copy(chol_hbm.at[pl.ds(group, 8)], cbuf.at[n], sem.at[0, n])
            two = pltpu.make_async_copy(cols_hbm.at[pl.ds(group, 8)], nbuf.at[n], sem.at[1, n])
            one.start()
            two.start()
            copies.append((one, two))
            where_row.append(row - group)
    for panel in range(2):
        for slot in range(SLOTS):
            n = panel * SLOTS + slot
            for copy in copies[n]:
                copy.wait()
            at = slot_base(panel, slot)
            sub = lax.broadcasted_iota(jnp.int32, (8, 128), 0) == where_row[n]
            for c in range(6 if panel == 0 else 7):
                tile = cbuf[n, :, c * 128 : c * 128 + 128] if c < 4 else nbuf[n, :, (c - 4) * 128 : (c - 3) * 128]
                out_ref[at + c : at + c + 1, :] = jnp.sum(jnp.where(sub, tile, 0.0), axis=0, keepdims=True)
    out_ref[39:40, :] = jnp.zeros((1, 128), F32)


def pick(pivots, chol_done, new_cols):
    return pl.pallas_call(
        pick_kernel,
        out_shape=jax.ShapeDtypeStruct((SLOT_ROWS, 128), F32),
        in_specs=[
            pl.BlockSpec(memory_space=pltpu.VMEM),
            pl.BlockSpec(memory_space=pl.ANY),
            pl.BlockSpec(memory_space=pl.ANY),
        ],
        out_specs=pl.BlockSpec(memory_space=pltpu.VMEM),
        scratch_shapes=[
            pltpu.VMEM((6, 8, K), F32),
            pltpu.VMEM((6, 8, COLS), F32),
            pltpu.SemaphoreType.DMA((2, 6)),
        ],
    )(pivots, chol_done, new_cols)


def gather_kernel(in_ref, g_ref, own_sem, send_sem, recv_sem, pass_send, pass_recv):
    grp, blk = lax.axis_index("grp"), lax.axis_index("blk")
    at = {"z": lax.div(grp, 2), "x": lax.div(blk, 4), "y": lax.rem(blk, 4)}
    core = lax.rem(grp, 2)

    def device(z, c, x, y):
        return (z * 2 + c, x * 4 + y)

    def beside(axis, k):
        there = dict(at)
        there[axis] = lax.rem(at[axis] + k, 4)
        return device(there["z"], core, there["x"], there["y"])

    partner = device(at["z"], 1 - core, at["x"], at["y"])
    barrier = pltpu.get_barrier_semaphore()
    for axis in "xyz":
        for k in (1, 2, 3):
            pl.semaphore_signal(barrier, inc=1, device_id=beside(axis, k), device_id_type=MESH)
    pl.semaphore_signal(barrier, inc=1, device_id=partner, device_id_type=MESH)
    own = pltpu.make_async_copy(in_ref, g_ref.at[at["z"], core, at["x"], at["y"]], own_sem)
    own.start()
    pl.semaphore_wait(barrier, 10)

    def region(colour, have, fixed):
        first, count, _ = COLOURS[colour]
        pick_at = [slice(None) if a in have else fixed[a] for a in "zxy"]
        return g_ref.at[pick_at[0], core, pick_at[1], pick_at[2], pl.ds(first, count), :]

    flights = {}

    def launch(colour, phase):
        first, count, order = COLOURS[colour]
        have = order[:phase]
        here = region(colour, have, at)
        for k in (2, 1, 3):
            source = in_ref.at[pl.ds(first, count), :] if phase == 0 else here
            copy = pltpu.make_async_remote_copy(
                src_ref=source,
                dst_ref=here,
                send_sem=send_sem.at[colour, phase, k - 1],
                recv_sem=recv_sem.at[colour, phase, k - 1],
                device_id=beside(order[phase], k),
                device_id_type=MESH,
            )
            copy.start()
            flights[colour, phase, k] = copy

    passes = []

    def hand_over(colour, piece, ref):
        copy = pltpu.make_async_remote_copy(
            src_ref=ref,
            dst_ref=ref,
            send_sem=pass_send.at[colour, piece],
            recv_sem=pass_recv.at[colour, piece],
            device_id=partner,
            device_id_type=MESH,
        )
        copy.start()
        passes.append(copy)

    colours = range(len(COLOURS))
    for colour in colours:
        launch(colour, 0)
    own.wait()
    for phase in (1, 2):
        for colour in colours:
            for k in (1, 3, 2):
                flights[colour, phase - 1, k].wait_recv()
            launch(colour, phase)
            if phase == 2:
                hand_over(colour, 0, region(colour, COLOURS[colour][2][:2], at))
    for k in (1, 3, 2):
        for colour in colours:
            flights[colour, 2, k].wait_recv()
            last = COLOURS[colour][2][2]
            there = dict(at)
            there[last] = lax.rem(at[last] + (4 - k), 4)
            hand_over(colour, k, region(colour, COLOURS[colour][2][:2], there))
    for copy in passes:
        copy.wait_recv()
    for copy in passes:
        copy.wait_send()
    for copy in flights.values():
        copy.wait_send()


def gather(slots):
    return pl.pallas_call(
        gather_kernel,
        out_shape=jax.ShapeDtypeStruct((4, 2, 4, 4, SLOT_ROWS, 128), F32),
        in_specs=[pl.BlockSpec(memory_space=pltpu.VMEM)],
        out_specs=pl.BlockSpec(memory_space=pltpu.VMEM),
        scratch_shapes=[
            pltpu.SemaphoreType.DMA,
            pltpu.SemaphoreType.DMA((3, 3, 3)),
            pltpu.SemaphoreType.DMA((3, 3, 3)),
            pltpu.SemaphoreType.DMA((3, 4)),
            pltpu.SemaphoreType.DMA((3, 4)),
        ],
        compiler_params=pltpu.CompilerParams(collective_id=0, has_side_effects=True),
    )(slots)


def split2(a):
    high = a.astype(BF16)
    return high, (a - high.astype(F32)).astype(BF16)


def split3(a):
    high = a.astype(BF16)
    rest = a - high.astype(F32)
    mid = rest.astype(BF16)
    return high, mid, (rest - mid.astype(F32)).astype(BF16)


def mul(a, b):
    return jnp.dot(a, b, preferred_element_type=F32)


def mul3(a, b_high, b_low):
    high, low = split2(a)
    return mul(high, b_high) + (mul(high, b_low) + mul(low, b_high))


def exact(a, b):
    return jnp.dot(a, b, precision=HIGHEST, preferred_element_type=F32)


def over_lanes(x, lane):
    return jnp.take_along_axis(x, jnp.full((8, 128), lane, jnp.int32), axis=1)


def over_rows(x, row):
    return jnp.broadcast_to(x[row : row + 1, :], (8, 128))


def factor_round(a_ref, r, off):
    rs = pl.multiple_of(r * STEP, STEP)
    c0 = off + r * STEP
    t = c0 // 128
    l0 = c0 - t * 128
    tl = pl.multiple_of(t * 128, 128)
    lane = lax.broadcasted_iota(jnp.int32, (8, 128), 1)
    sub = lax.broadcasted_iota(jnp.int32, (8, 128), 0)
    raw = [a_ref[pl.ds(rs + 8 * q, 8), pl.ds(tl, 128)] for q in range(2)]
    col = {}
    for j in range(STEP):
        for q in range(j // 8, 2):
            col[j, q] = over_lanes(raw[q], l0 + j)
    row = {}
    for q in range(2):
        for h in range(2):
            x = a_ref[pl.ds(rs + 8 * q, 8), h * 128 : (h + 1) * 128]
            rel = lane + (h * 128) - c0
            unit = jnp.where(rel == sub + 8 * q, 1.0, 0.0)
            row[q, h] = jnp.where((rel >= 0) & (rel < STEP), unit, x)
    for j in range(STEP):
        jq, js = j // 8, j % 8
        scale = lax.rsqrt(over_rows(col[j, jq], js))
        low = {q: col[j, q] * scale for q in range(jq, 2)}
        for m in range(j + 1, STEP):
            times = over_rows(low[m // 8], m % 8)
            for q in range(m // 8, 2):
                col[m, q] = col[m, q] - low[q] * times
        low[jq] = jnp.where(sub > js, low[jq], 0.0)
        for h in range(2):
            lead = over_rows(row[jq, h], js) * scale
            for q in range(jq, 2):
                row[q, h] = row[q, h] - low[q] * lead
            row[jq, h] = jnp.where(sub == js, lead, row[jq, h])
    for q in range(2):
        for h in range(2):
            a_ref[pl.ds(rs + 8 * q, 8), h * 128 : (h + 1) * 128] = row[q, h]
    u = jnp.concatenate([jnp.concatenate([row[q, h] for h in range(2)], axis=1) for q in range(2)], axis=0)
    lanes = lax.broadcasted_iota(jnp.int32, (STEP, 256), 1)
    high, mid, low3 = split3(u)
    zero = jnp.zeros_like(u)
    ahead = lanes >= c0 + STEP
    h_l, m_l, l_l = split3(jnp.where(ahead, u, zero))
    left = jnp.concatenate([h_l, h_l, m_l, m_l, h_l, l_l], axis=0)
    right = jnp.concatenate([high, mid, high, mid, low3, high], axis=0)
    z = lax.dot_general(left, right, (((0,), (0,)), ((), ())), preferred_element_type=F32)
    rows_i = lax.broadcasted_iota(jnp.int32, (ORDER, 256), 0)
    cols_i = lax.broadcasted_iota(jnp.int32, (ORDER, 256), 1)
    old = (rows_i >= rs + STEP) & (cols_i >= c0) & (cols_i < c0 + STEP)
    a_ref[...] = jnp.where(old, 0.0, a_ref[...]) - z[off : off + ORDER, :]


def lower_only(a, off):
    row = lax.broadcasted_iota(jnp.int32, (ORDER, 256), 0)
    col = lax.broadcasted_iota(jnp.int32, (ORDER, 256), 1) - off
    return jnp.where((col >= 0) & (col <= row), a, 0.0)


def panel_kernel(g_ref, piv_ref, live_ref, diag_ref, chol_hbm, cols_hbm, out_hbm, top_ref,
                 chol, rbuf, squares, hmat, htr, ht_high, ht_low, head, a_ref,
                 v_high, v_low, f_high, f_low, sums, in_sem, out_sem):
    me = lax.axis_index("grp") * 16 + lax.axis_index("blk")
    alive = live_ref[me] * BLOCK_ROWS

    def fetch(start, count, n):
        rows = pl.ds(start, count)
        return (
            pltpu.make_async_copy(chol_hbm.at[rows], chol.at[rows], in_sem.at[0, n]),
            pltpu.make_async_copy(cols_hbm.at[rows], rbuf.at[rows], in_sem.at[1, n]),
        )

    for n, (start, count) in enumerate(CHUNKS):
        for copy in fetch(start, count, n):
            copy.start()

    q_i = lax.broadcasted_iota(jnp.int32, (ORDER, ORDER), 1)
    p_i = lax.broadcasted_iota(jnp.int32, (ORDER, ORDER), 0)
    for panel in range(2):
        owner_row = (piv_ref[panel : panel + 1, :] // ROWS).astype(F32)
        owner_all = jnp.broadcast_to(owner_row, (ORDER, ORDER))
        owner = jnp.sum(jnp.where(q_i == p_i, owner_all, 0.0), axis=1, keepdims=True)
        before = (owner_all == owner) & (q_i < p_i)
        rank = jnp.sum(jnp.where(before, 1.0, 0.0), axis=1, keepdims=True)
        dev = lax.broadcasted_iota(jnp.int32, (ORDER, 128), 1).astype(F32)
        hot = jnp.concatenate(
            [jnp.where((dev == owner) & (rank == float(s)), 1.0, 0.0) for s in range(SLOTS)], axis=1
        ).astype(BF16)
        for c in range(6 if panel == 0 else 7):
            pieces = [g_ref[pl.ds(slot_base(panel, s) + c, 128, stride=SLOT_ROWS), :] for s in range(SLOTS)]
            high, mid, low = split3(jnp.concatenate(pieces, axis=0))
            rows = mul(hot, high) + (mul(hot, mid) + mul(hot, low))
            if c < 4:
                hmat[panel * ORDER : (panel + 1) * ORDER, c * 128 : (c + 1) * 128] = rows
            else:
                head[panel, :, (c - 4) * 128 : (c - 3) * 128] = rows
    htr[...] = hmat[...].T
    high, low = split2(htr[...])
    ht_high[...] = high
    ht_low[...] = low

    lanes = lax.broadcasted_iota(jnp.int32, (ORDER, 256), 1)
    one = head[0, :, 0:256] - exact(hmat[0:ORDER, :], htr[:, 0:256])
    a_ref[...] = jnp.where(lanes < ORDER, one, 0.0)

    def residual(start, count):
        rows = pl.ds(start, count)
        tile = chol[rows, :]
        left = rbuf[rows, :] - mul3(tile, ht_high[...], ht_low[...])
        spot = lax.broadcasted_iota(jnp.int32, (count, COLS), 0) + start
        rbuf[rows, :] = jnp.where(spot < alive, left, 0.0)
        square = tile * tile
        squares[rows, :] = (square[:, 0:128] + square[:, 128:256]) + (square[:, 256:384] + square[:, 384:512])

    def round_one(r, _):
        start = pl.multiple_of(r * TILE, TILE)
        for copy in fetch(start, TILE, r):
            copy.wait()
        factor_round(a_ref, r, 0)
        residual(start, TILE)
        return 0

    lax.fori_loop(0, ROUNDS, round_one, 0)
    for copy in fetch(ROUNDS * TILE, LAST, ROUNDS):
        copy.wait()
    residual(ROUNDS * TILE, LAST)

    pad = jnp.zeros((64, 256), F32)
    v_one = jnp.concatenate([lower_only(a_ref[...], 0), pad], axis=0).T
    high, low = split2(v_one)
    v_high[...] = high
    v_low[...] = low
    cross = head[1, :, 0:256] - exact(hmat[ORDER:, :], htr[:, 0:256])
    f_rows = exact(cross, v_one)
    f_tr = jnp.concatenate([pad, f_rows], axis=0).T
    high, low = split2(f_tr)
    f_high[...] = high
    f_low[...] = low
    two = (head[1, :, 128:384] - exact(hmat[ORDER:, :], htr[:, 128:384])) - exact(f_rows, f_tr)
    a_ref[...] = jnp.where(lanes >= 64, two, 0.0)

    def first_of(start, count):
        rows = pl.ds(start, count)
        first = mul3(rbuf[rows, 0:256], v_high[...], v_low[...])
        rest = rbuf[rows, 128:384] - mul3(first, f_high[...], f_low[...])
        rbuf[rows, 0:128] = first[:, 0:128]
        spot = lax.broadcasted_iota(jnp.int32, (count, 128), 1)
        rbuf[rows, 128:256] = jnp.where(spot < 64, first[:, 128:256], rest[:, 0:128])
        rbuf[rows, 256:384] = rest[:, 128:256]
        squares[rows, :] = squares[rows, :] + (first[:, 0:128] * first[:, 0:128] + first[:, 128:256] * first[:, 128:256])

    def round_two(r, _):
        factor_round(a_ref, r, 64)
        first_of(pl.multiple_of(r * TILE, TILE), TILE)
        return 0

    lax.fori_loop(0, ROUNDS, round_two, 0)
    first_of(ROUNDS * TILE, LAST)

    v_two = jnp.concatenate([pad, lower_only(a_ref[...], 64)], axis=0).T
    high, low = split2(v_two)
    v_high[...] = high
    v_low[...] = low

    def send(start, count, n):
        rows = pl.ds(start, count)
        return pltpu.make_async_copy(rbuf.at[rows], out_hbm.at[rows], out_sem.at[n])

    def second_of(start, count, n, at):
        rows = pl.ds(start, count)
        second = mul3(rbuf[rows, 128:384], v_high[...], v_low[...])
        spot = lax.broadcasted_iota(jnp.int32, (count, 128), 1)
        rbuf[rows, 128:256] = jnp.where(spot < 64, rbuf[rows, 128:256], second[:, 0:128])
        rbuf[rows, 256:384] = second[:, 128:256]
        send(start, count, n).start()
        square = squares[rows, :] + (second[:, 0:128] * second[:, 0:128] + second[:, 128:256] * second[:, 128:256])
        ones = jnp.ones((8, 128), F32)
        total = lax.dot_general(ones, square, (((1,), (1,)), ((), ())), precision=HIGHEST, preferred_element_type=F32)
        for q in range(count // 128):
            sums[pl.ds(at + q, 1), :] = total[0:1, q * 128 : (q + 1) * 128]

    def round_three(r, _):
        second_of(pl.multiple_of(r * TILE, TILE), TILE, r, r * (TILE // 128))
        return 0

    lax.fori_loop(0, ROUNDS, round_three, 0)
    second_of(ROUNDS * TILE, LAST, ROUNDS, ROUNDS * TILE // 128)

    entry = lax.broadcasted_iota(jnp.int32, (38, 128), 0) * 128 + lax.broadcasted_iota(jnp.int32, (38, 128), 1)
    live = jnp.where(entry < alive, 1.0, 0.0)
    left = live * (diag_ref[...] - sums[...])
    top_left = jnp.max(left)
    top_diag = jnp.max(live * diag_ref[...])
    spot = lax.broadcasted_iota(jnp.int32, (1, 128), 1)
    top_ref[...] = jnp.where(spot < 64, top_left, top_diag)
    for n, (start, count) in enumerate(CHUNKS):
        send(start, count, n).wait()


def panels(everybody, pivots, live_blocks, diag, chol_done, new_cols):
    vmem = pl.BlockSpec(memory_space=pltpu.VMEM)
    hbm = pl.BlockSpec(memory_space=pl.ANY)
    return pl.pallas_call(
        panel_kernel,
        out_shape=(jax.ShapeDtypeStruct((ROWS, COLS), F32), jax.ShapeDtypeStruct((1, 128), F32)),
        in_specs=[vmem, vmem, pl.BlockSpec(memory_space=pltpu.SMEM), vmem, hbm, hbm],
        out_specs=(hbm, vmem),
        scratch_shapes=[
            pltpu.VMEM((ROWS, K), F32),
            pltpu.VMEM((ROWS, COLS), F32),
            pltpu.VMEM((ROWS, 128), F32),
            pltpu.VMEM((COLS, K), F32),
            pltpu.VMEM((K, COLS), F32),
            pltpu.VMEM((K, COLS), BF16),
            pltpu.VMEM((K, COLS), BF16),
            pltpu.VMEM((2, ORDER, COLS), F32),
            pltpu.VMEM((ORDER, 256), F32),
            pltpu.VMEM((256, 256), BF16),
            pltpu.VMEM((256, 256), BF16),
            pltpu.VMEM((256, 256), BF16),
            pltpu.VMEM((256, 256), BF16),
            pltpu.VMEM((38, 128), F32),
            pltpu.SemaphoreType.DMA((2, ROUNDS + 1)),
            pltpu.SemaphoreType.DMA((ROUNDS + 1,)),
        ],
        compiler_params=pltpu.CompilerParams(vmem_limit_bytes=VMEM_LIMIT),
    )(everybody, pivots, live_blocks, diag, chol_done, new_cols)


def top_kernel(in_ref, out_ref, table, own_sem, near_send, near_recv, far_send, far_recv):
    grp, blk = lax.axis_index("grp"), lax.axis_index("blk")
    barrier = pltpu.get_barrier_semaphore()
    near = [(lax.rem(grp + k, 8), blk) for k in range(1, 8)]
    far = [(grp, lax.rem(blk + k, 16)) for k in range(1, 16)]
    for there in near + far:
        pl.semaphore_signal(barrier, inc=1, device_id=there, device_id_type=MESH)
    mine = table.at[blk, grp]
    own = pltpu.make_async_copy(in_ref, mine, own_sem)
    own.start()
    pl.semaphore_wait(barrier, len(near) + len(far))
    one = []
    for n, there in enumerate(near):
        copy = pltpu.make_async_remote_copy(
            src_ref=in_ref, dst_ref=mine, send_sem=near_send.at[n], recv_sem=near_recv.at[n],
            device_id=there, device_id_type=MESH,
        )
        copy.start()
        one.append(copy)
    own.wait()
    for copy in one:
        copy.wait_recv()
    two = []
    for n, there in enumerate(far):
        copy = pltpu.make_async_remote_copy(
            src_ref=table.at[blk], dst_ref=table.at[blk], send_sem=far_send.at[n], recv_sem=far_recv.at[n],
            device_id=there, device_id_type=MESH,
        )
        copy.start()
        two.append(copy)
    for copy in two:
        copy.wait_recv()
    best = jnp.max(table[...].reshape(128, 128), axis=0, keepdims=True)
    spot = lax.broadcasted_iota(jnp.int32, (1, 128), 1)
    low = -3.0e38
    left = jnp.max(jnp.where(spot < 64, best, low), axis=1, keepdims=True)
    diag = jnp.max(jnp.where(spot < 64, low, best), axis=1, keepdims=True)
    out_ref[...] = jnp.broadcast_to(left / diag, (1, 128))
    for copy in one + two:
        copy.wait_send()


def top(mine):
    return pl.pallas_call(
        top_kernel,
        out_shape=jax.ShapeDtypeStruct((1, 128), F32),
        in_specs=[pl.BlockSpec(memory_space=pltpu.VMEM)],
        out_specs=pl.BlockSpec(memory_space=pltpu.VMEM),
        scratch_shapes=[
            pltpu.VMEM((16, 8, 1, 128), F32),
            pltpu.SemaphoreType.DMA,
            pltpu.SemaphoreType.DMA((7,)),
            pltpu.SemaphoreType.DMA((7,)),
            pltpu.SemaphoreType.DMA((15,)),
            pltpu.SemaphoreType.DMA((15,)),
        ],
        compiler_params=pltpu.CompilerParams(collective_id=1, has_side_effects=True),
    )(mine)


def body(chol_done, new_cols, diag_entries, pivots, live_blocks):
    slots = pick(pivots, chol_done, new_cols)
    everybody = gather(slots).reshape(128 * SLOT_ROWS, 128)
    diag = diag_entries.reshape(ROWS // 128, 128)
    vectors, mine = panels(everybody, pivots, live_blocks, diag, chol_done, new_cols)
    return vectors, top(mine)[0, 0:1]


def solution(mesh):
    placed = (P(("grp", "blk"), None), P(("grp", "blk"), None), P(("grp", "blk")), P(), P())
    return jax.shard_map(
        body, mesh=mesh, in_specs=placed, out_specs=(P(("grp", "blk"), None), P()), check_vma=False
    )
```

time: 592 us -> 89 us (0.15); the launches traced: 582 us -> 88.8 us
  waiting for transfers between devices: 282 us -> 0 us
  other arithmetic: 112 us -> 0 us
  Pallas kernels: 0 us -> 86.5 us
  blocking collectives: 63.6 us -> 0 us
  matrix products: 60.4 us -> 0 us
  local copies, waits for them, and re-layouts: 44.3 us -> 0 us
  between operations: 20.4 us -> 2.34 us
    psum x2 -> x0, waiting for transfers between devices: 282 us -> none  [collect(): return lax.psum(parts, ('grp', 'blk'))]
    another operation x24 -> x0, other arithmetic: 97.5 us -> none  [the longest x14 57.5 us: factor_inverse(): lower = jnp.linalg.cholesky(block)]
    pallas_call x0 -> x4, Pallas kernels: none -> 86.5 us  [the longest x1 46 us: panels(): pl.pallas_call(panel_kernel, out_shape=(jax.ShapeDtypeStruct((ROWS, COLS)...]
    pmax x1 -> x0, blocking collectives: 63.6 us -> none  [body(): lax.pmax((jnp.max(left), jnp.max(diag_entries * mask)), ('grp', 'blk'))]
    dot_general x8 -> x0, matrix products: 57.5 us -> none  [the longest x3 39.5 us: local_panel(): resid = resid - jnp.dot(factor, head.T, precision=lax.Precision.HIGHEST)]
    gather x8 -> x0, local copies, waits for them, and re-layouts: 19.9 us -> none  [collect(): source[safe]]
    slice x1 -> x0, local copies, waits for them, and re-layouts: 9.14 us -> none  [body(): cols_second = new_cols[:, order:]]
    unnamed x11 -> x0, local copies, waits for them, and re-layouts: 8.58 us -> none
  transfers between devices with their start and end apart: 2 -> 0, of which waited for: 2 -> 0; matrix products, arithmetic and copies ran while one was open for 2% -> 0% of each run, Pallas kernels for 0% -> 0%
where the time goes in v1:
time: 89 us; the launch traced here: 88.8 us
  Pallas kernels  86.5 us (97%)
  between operations  2.34 us (3%)
    pallas_call x1, Pallas kernels, panels(): pl.pallas_call(panel_kernel, out_shape=(jax.ShapeDtypeStruct((ROWS, COLS)...  46 us
    pallas_call x1, Pallas kernels, gather(): pl.pallas_call(gather_kernel, out_shape=jax.ShapeDtypeStruct((4, 2, 4, 4,...  25 us
    pallas_call x1, Pallas kernels, top(): pl.pallas_call(top_kernel, out_shape=jax.ShapeDtypeStruct((1, 128), F32),...  13 us
    pallas_call x1, Pallas kernels, pick(): pl.pallas_call(pick_kernel, out_shape=jax.ShapeDtypeStruct((SLOT_ROWS, 12...  2.53 us

profile of v1, /device:TPU:0, one launch (start us, length us, event | category | flops | bytes accessed | tf_op | source)
XLA Modules:
  0.0 88.8 jit_solution(1140485190509860071)
XLA Ops:
  0.6 2.5 %shard_map.68.in_ref = f32[40,128]{1,0:T(8,128)} custom-call(s32[2,192]{1,0:T(2,128)} %piv_ref.3, f32[4864,512]{1,0:T(8,128)} %chol_hbm.3, f32[4864,384]{1,0:T(8,128)} %cols_hbm.3), custom_call_target="tpu_custom_call" | custom-call | tf_op jit(solution)/shard_map/pallas_call | solution.py:73
  3.2 25.0 %shard_map.69 = f32[4,2,4,4,40,128]{5,4,3,2,1,0:T(8,128)} custom-call(f32[40,128]{1,0:T(8,128)} %shard_map.68.in_ref), custom_call_target="tpu_custom_call" | custom-call | tf_op jit(solution)/shard_map/pallas_call | solution.py:178
  28.2 46.0 %shard_map.70 = (f32[4864,384]{1,0:T(8,128)}, f32[1,128]{1,0:T(1,128)}) custom-call(f32[5120,128]{1,0:T(8,128)} %bitcast.4, s32[2,192]{1,0:T(2,128)} %piv_ref.3, s32[128]{0:T(128)} %live_ref.1, f32[38,128]{1,0:T(8,128)} %bitcast.5, f32[4864,512]{1,0:T(8,128)} %chol_hbm.3, f32[4864,384]{1,0:T(8,128)} %cols_hbm.3), custom_call_target="tpu_custom_call" | custom-call | tf_op jit(solution)/shard_map/pallas_call | solution.py:428
  74.1 13.0 %shard_map.71 = f32[1,128]{1,0:T(1,128)} custom-call(f32[1,128]{1,0:T(1,128)} %get-tuple-element.5.in_ref), custom_call_target="tpu_custom_call" | custom-call | tf_op jit(solution)/shard_map/pallas_call | solution.py:498

commit v2 on v1

--- a/solution.py
+++ b/solution.py
@@ -21,6 +21,7 @@
 TILE = 384
 LAST = ROWS - ROUNDS * TILE
 CHUNKS = [(i * TILE, TILE) for i in range(ROUNDS)] + [(ROUNDS * TILE, LAST)]
+BIG = 768
 VMEM_LIMIT = 60 * 1024 * 1024
 COLOURS = ((0, 16, "yxz"), (16, 16, "xzy"), (32, 8, "zyx"))
 
@@ -284,7 +285,7 @@
 
 def panel_kernel(g_ref, piv_ref, live_ref, diag_ref, chol_hbm, cols_hbm, out_hbm, top_ref,
                  chol, rbuf, squares, hmat, htr, ht_high, ht_low, head, a_ref,
-                 v_high, v_low, f_high, f_low, sums, in_sem, out_sem):
+                 v_high, v_low, w_high, w_low, sums, in_sem, out_sem):
     me = lax.axis_index("grp") * 16 + lax.axis_index("blk")
     alive = live_ref[me] * BLOCK_ROWS
 
@@ -341,8 +342,8 @@
         start = pl.multiple_of(r * TILE, TILE)
         for copy in fetch(start, TILE, r):
             copy.wait()
+        residual(start, TILE)
         factor_round(a_ref, r, 0)
-        residual(start, TILE)
         return 0
 
     lax.fori_loop(0, ROUNDS, round_one, 0)
@@ -352,22 +353,20 @@
 
     pad = jnp.zeros((64, 256), F32)
     v_one = jnp.concatenate([lower_only(a_ref[...], 0), pad], axis=0).T
-    high, low = split2(v_one)
-    v_high[...] = high
-    v_low[...] = low
     cross = head[1, :, 0:256] - exact(hmat[ORDER:, :], htr[:, 0:256])
     f_rows = exact(cross, v_one)
     f_tr = jnp.concatenate([pad, f_rows], axis=0).T
-    high, low = split2(f_tr)
-    f_high[...] = high
-    f_low[...] = low
+    high, low = split2(jnp.concatenate([v_one, exact(v_one, f_tr)], axis=1))
+    w_high[...] = high
+    w_low[...] = low
     two = (head[1, :, 128:384] - exact(hmat[ORDER:, :], htr[:, 128:384])) - exact(f_rows, f_tr)
     a_ref[...] = jnp.where(lanes >= 64, two, 0.0)
 
     def first_of(start, count):
         rows = pl.ds(start, count)
-        first = mul3(rbuf[rows, 0:256], v_high[...], v_low[...])
-        rest = rbuf[rows, 128:384] - mul3(first, f_high[...], f_low[...])
+        both = mul3(rbuf[rows, 0:256], w_high[...], w_low[...])
+        first = both[:, 0:256]
+        rest = rbuf[rows, 128:384] - both[:, 256:512]
         rbuf[rows, 0:128] = first[:, 0:128]
         spot = lax.broadcasted_iota(jnp.int32, (count, 128), 1)
         rbuf[rows, 128:256] = jnp.where(spot < 64, first[:, 128:256], rest[:, 0:128])
@@ -375,8 +374,8 @@
         squares[rows, :] = squares[rows, :] + (first[:, 0:128] * first[:, 0:128] + first[:, 128:256] * first[:, 128:256])
 
     def round_two(r, _):
+        first_of(pl.multiple_of(r * TILE, TILE), TILE)
         factor_round(a_ref, r, 64)
-        first_of(pl.multiple_of(r * TILE, TILE), TILE)
         return 0
 
     lax.fori_loop(0, ROUNDS, round_two, 0)
@@ -399,17 +398,16 @@
         rbuf[rows, 256:384] = second[:, 128:256]
         send(start, count, n).start()
         square = squares[rows, :] + (second[:, 0:128] * second[:, 0:128] + second[:, 128:256] * second[:, 128:256])
-        ones = jnp.ones((8, 128), F32)
-        total = lax.dot_general(ones, square, (((1,), (1,)), ((), ())), precision=HIGHEST, preferred_element_type=F32)
         for q in range(count // 128):
-            sums[pl.ds(at + q, 1), :] = total[0:1, q * 128 : (q + 1) * 128]
+            turned = square[q * 128 : (q + 1) * 128, :].T
+            sums[pl.ds(at + q, 1), :] = jnp.sum(turned, axis=0, keepdims=True)
 
     def round_three(r, _):
-        second_of(pl.multiple_of(r * TILE, TILE), TILE, r, r * (TILE // 128))
+        second_of(pl.multiple_of(r * BIG, BIG), BIG, r, r * (BIG // 128))
         return 0
 
-    lax.fori_loop(0, ROUNDS, round_three, 0)
-    second_of(ROUNDS * TILE, LAST, ROUNDS, ROUNDS * TILE // 128)
+    lax.fori_loop(0, ROWS // BIG, round_three, 0)
+    second_of(ROWS // BIG * BIG, ROWS % BIG, ROWS // BIG, ROWS // BIG * BIG // 128)
 
     entry = lax.broadcasted_iota(jnp.int32, (38, 128), 0) * 128 + lax.broadcasted_iota(jnp.int32, (38, 128), 1)
     live = jnp.where(entry < alive, 1.0, 0.0)
@@ -418,8 +416,9 @@
     top_diag = jnp.max(live * diag_ref[...])
     spot = lax.broadcasted_iota(jnp.int32, (1, 128), 1)
     top_ref[...] = jnp.where(spot < 64, top_left, top_diag)
-    for n, (start, count) in enumerate(CHUNKS):
-        send(start, count, n).wait()
+    for n in range(ROWS // BIG):
+        send(n * BIG, BIG, n).wait()
+    send(ROWS // BIG * BIG, ROWS % BIG, ROWS // BIG).wait()
 
 
 def panels(everybody, pivots, live_blocks, diag, chol_done, new_cols):
@@ -442,8 +441,8 @@
             pltpu.VMEM((ORDER, 256), F32),
             pltpu.VMEM((256, 256), BF16),
             pltpu.VMEM((256, 256), BF16),
-            pltpu.VMEM((256, 256), BF16),
-            pltpu.VMEM((256, 256), BF16),
+            pltpu.VMEM((256, 512), BF16),
+            pltpu.VMEM((256, 512), BF16),
             pltpu.VMEM((38, 128), F32),
             pltpu.SemaphoreType.DMA((2, ROUNDS + 1)),
             pltpu.SemaphoreType.DMA((ROUNDS + 1,)),

time: 89 us -> 71.7 us (0.81)
  Pallas kernels: 86.5 us -> 68.9 us
    pallas_call x1, Pallas kernels: 46 us -> 28.6 us  [panels(): pl.pallas_call(panel_kernel, out_shape=(jax.ShapeDtypeStruct((ROWS, COLS)...]
where the time goes in v2:
time: 71.7 us; the launch traced here: 71.3 us
  Pallas kernels  68.9 us (96%)
  between operations  2.34 us (3%)
    pallas_call x1, Pallas kernels, panels(): pl.pallas_call(panel_kernel, out_shape=(jax.ShapeDtypeStruct((ROWS, COLS)...  28.6 us
    pallas_call x1, Pallas kernels, gather(): pl.pallas_call(gather_kernel, out_shape=jax.ShapeDtypeStruct((4, 2, 4, 4,...  25 us
    pallas_call x1, Pallas kernels, top(): pl.pallas_call(top_kernel, out_shape=jax.ShapeDtypeStruct((1, 128), F32),...  12.8 us
    pallas_call x1, Pallas kernels, pick(): pl.pallas_call(pick_kernel, out_shape=jax.ShapeDtypeStruct((SLOT_ROWS, 12...  2.53 us

profile of v2, /device:TPU:0, one launch (start us, length us, event | category | flops | bytes accessed | tf_op | source)
XLA Modules:
  0.0 71.3 jit_solution(977877305598099214)
XLA Ops:
  0.6 2.5 %shard_map.68.in_ref = f32[40,128]{1,0:T(8,128)} custom-call(s32[2,192]{1,0:T(2,128)} %piv_ref.3, f32[4864,512]{1,0:T(8,128)} %chol_hbm.3, f32[4864,384]{1,0:T(8,128)} %cols_hbm.3), custom_call_target="tpu_custom_call" | custom-call | tf_op jit(solution)/shard_map/pallas_call | solution.py:74
  3.2 25.0 %shard_map.69 = f32[4,2,4,4,40,128]{5,4,3,2,1,0:T(8,128)} custom-call(f32[40,128]{1,0:T(8,128)} %shard_map.68.in_ref), custom_call_target="tpu_custom_call" | custom-call | tf_op jit(solution)/shard_map/pallas_call | solution.py:179
  28.2 28.6 %shard_map.70 = (f32[4864,384]{1,0:T(8,128)}, f32[1,128]{1,0:T(1,128)}) custom-call(f32[5120,128]{1,0:T(8,128)} %bitcast.4, s32[2,192]{1,0:T(2,128)} %piv_ref.3, s32[128]{0:T(128)} %live_ref.1, f32[38,128]{1,0:T(8,128)} %bitcast.5, f32[4864,512]{1,0:T(8,128)} %chol_hbm.3, f32[4864,384]{1,0:T(8,128)} %cols_hbm.3), custom_call_target="tpu_custom_call" | custom-call | tf_op jit(solution)/shard_map/pallas_call | solution.py:427
  56.8 12.8 %shard_map.71 = f32[1,128]{1,0:T(1,128)} custom-call(f32[1,128]{1,0:T(1,128)} %get-tuple-element.5.in_ref), custom_call_target="tpu_custom_call" | custom-call | tf_op jit(solution)/shard_map/pallas_call | solution.py:497

commit v3 on v2

--- a/solution.py
+++ b/solution.py
@@ -18,11 +18,10 @@
 SLOT_ROWS = 40
 STEP = 16
 ROUNDS = ORDER // STEP
+BIG = 768
 TILE = 384
-LAST = ROWS - ROUNDS * TILE
-CHUNKS = [(i * TILE, TILE) for i in range(ROUNDS)] + [(ROUNDS * TILE, LAST)]
-BIG = 768
-VMEM_LIMIT = 60 * 1024 * 1024
+CHUNKS = [(i * BIG, BIG) for i in range(ROWS // BIG)] + [(ROWS // BIG * BIG, ROWS % BIG)]
+VMEM_LIMIT = 24 * 1024 * 1024
 COLOURS = ((0, 16, "yxz"), (16, 16, "xzy"), (32, 8, "zyx"))
 
 
@@ -76,8 +75,8 @@
         out_shape=jax.ShapeDtypeStruct((SLOT_ROWS, 128), F32),
         in_specs=[
             pl.BlockSpec(memory_space=pltpu.VMEM),
-            pl.BlockSpec(memory_space=pl.ANY),
-            pl.BlockSpec(memory_space=pl.ANY),
+            pl.BlockSpec(memory_space=pltpu.HBM),
+            pl.BlockSpec(memory_space=pltpu.HBM),
         ],
         out_specs=pl.BlockSpec(memory_space=pltpu.VMEM),
         scratch_shapes=[
@@ -85,6 +84,7 @@
             pltpu.VMEM((6, 8, COLS), F32),
             pltpu.SemaphoreType.DMA((2, 6)),
         ],
+        compiler_params=pltpu.CompilerParams(vmem_limit_bytes=60 * 1024 * 1024),
     )(pivots, chol_done, new_cols)
 
 
@@ -188,7 +188,8 @@
             pltpu.SemaphoreType.DMA((3, 4)),
             pltpu.SemaphoreType.DMA((3, 4)),
         ],
-        compiler_params=pltpu.CompilerParams(collective_id=0, has_side_effects=True),
+        compiler_params=pltpu.CompilerParams(collective_id=0, has_side_effects=True, vmem_limit_bytes=4 * 1024 * 1024),
+        cost_estimate=pl.CostEstimate(flops=20_000_000_000, bytes_accessed=2_700_000, transcendentals=0),
     )(slots)
 
 
@@ -283,22 +284,11 @@
     return jnp.where((col >= 0) & (col <= row), a, 0.0)
 
 
-def panel_kernel(g_ref, piv_ref, live_ref, diag_ref, chol_hbm, cols_hbm, out_hbm, top_ref,
-                 chol, rbuf, squares, hmat, htr, ht_high, ht_low, head, a_ref,
-                 v_high, v_low, w_high, w_low, sums, in_sem, out_sem):
+def panel_kernel(g_ref, piv_ref, live_ref, diag_ref, chol, cols, out_hbm, top_ref,
+                 rbuf, squares, hmat, htr, ht_pair, head, a_ref,
+                 v_high, v_low, w_pair, sums, out_sem):
     me = lax.axis_index("grp") * 16 + lax.axis_index("blk")
     alive = live_ref[me] * BLOCK_ROWS
-
-    def fetch(start, count, n):
-        rows = pl.ds(start, count)
-        return (
-            pltpu.make_async_copy(chol_hbm.at[rows], chol.at[rows], in_sem.at[0, n]),
-            pltpu.make_async_copy(cols_hbm.at[rows], rbuf.at[rows], in_sem.at[1, n]),
-        )
-
-    for n, (start, count) in enumerate(CHUNKS):
-        for copy in fetch(start, count, n):
-            copy.start()
 
     q_i = lax.broadcasted_iota(jnp.int32, (ORDER, ORDER), 1)
     p_i = lax.broadcasted_iota(jnp.int32, (ORDER, ORDER), 0)
@@ -321,50 +311,55 @@
             else:
                 head[panel, :, (c - 4) * 128 : (c - 3) * 128] = rows
     htr[...] = hmat[...].T
-    high, low = split2(htr[...])
-    ht_high[...] = high
-    ht_low[...] = low
-
     lanes = lax.broadcasted_iota(jnp.int32, (ORDER, 256), 1)
     one = head[0, :, 0:256] - exact(hmat[0:ORDER, :], htr[:, 0:256])
     a_ref[...] = jnp.where(lanes < ORDER, one, 0.0)
-
-    def residual(start, count):
+    head[1, :, :] = head[1, :, :] - exact(hmat[ORDER:, :], htr[...])
+    high, low = split2(htr[...])
+    ht_pair[:, 0:COLS] = high
+    ht_pair[:, COLS:] = low
+
+    def residual_high(start, count):
+        rows = pl.ds(start, count)
+        both = mul(chol[rows, :].astype(BF16), ht_pair[...])
+        rbuf[rows, :] = cols[rows, :] - (both[:, 0:COLS] + both[:, COLS:])
+
+    def residual_low(start, count):
         rows = pl.ds(start, count)
         tile = chol[rows, :]
-        left = rbuf[rows, :] - mul3(tile, ht_high[...], ht_low[...])
+        left = rbuf[rows, :] - mul(split2(tile)[1], ht_pair[:, 0:COLS])
         spot = lax.broadcasted_iota(jnp.int32, (count, COLS), 0) + start
         rbuf[rows, :] = jnp.where(spot < alive, left, 0.0)
         square = tile * tile
         squares[rows, :] = (square[:, 0:128] + square[:, 128:256]) + (square[:, 256:384] + square[:, 384:512])
 
     def round_one(r, _):
-        start = pl.multiple_of(r * TILE, TILE)
-        for copy in fetch(start, TILE, r):
-            copy.wait()
-        residual(start, TILE)
-        factor_round(a_ref, r, 0)
+        start = pl.multiple_of(r * BIG, BIG)
+        residual_high(start, BIG)
+        factor_round(a_ref, 2 * r, 0)
+        residual_low(start, BIG)
+        factor_round(a_ref, 2 * r + 1, 0)
         return 0
 
-    lax.fori_loop(0, ROUNDS, round_one, 0)
-    for copy in fetch(ROUNDS * TILE, LAST, ROUNDS):
-        copy.wait()
-    residual(ROUNDS * TILE, LAST)
+    lax.fori_loop(0, ROUNDS // 2, round_one, 0)
+    residual_high(*CHUNKS[-1])
+    residual_low(*CHUNKS[-1])
 
     pad = jnp.zeros((64, 256), F32)
     v_one = jnp.concatenate([lower_only(a_ref[...], 0), pad], axis=0).T
-    cross = head[1, :, 0:256] - exact(hmat[ORDER:, :], htr[:, 0:256])
-    f_rows = exact(cross, v_one)
+    f_rows = exact(head[1, :, 0:256], v_one)
     f_tr = jnp.concatenate([pad, f_rows], axis=0).T
+    two = head[1, :, 128:384] - exact(f_rows, f_tr)
+    a_ref[...] = jnp.where(lanes >= 64, two, 0.0)
     high, low = split2(jnp.concatenate([v_one, exact(v_one, f_tr)], axis=1))
-    w_high[...] = high
-    w_low[...] = low
-    two = (head[1, :, 128:384] - exact(hmat[ORDER:, :], htr[:, 128:384])) - exact(f_rows, f_tr)
-    a_ref[...] = jnp.where(lanes >= 64, two, 0.0)
+    w_pair[:, 0:512] = high
+    w_pair[:, 512:] = low
 
     def first_of(start, count):
         rows = pl.ds(start, count)
-        both = mul3(rbuf[rows, 0:256], w_high[...], w_low[...])
+        high, low = split2(rbuf[rows, 0:256])
+        wide = mul(high, w_pair[...])
+        both = (wide[:, 0:512] + wide[:, 512:]) + mul(low, w_pair[:, 0:512])
         first = both[:, 0:256]
         rest = rbuf[rows, 128:384] - both[:, 256:512]
         rbuf[rows, 0:128] = first[:, 0:128]
@@ -379,7 +374,7 @@
         return 0
 
     lax.fori_loop(0, ROUNDS, round_two, 0)
-    first_of(ROUNDS * TILE, LAST)
+    first_of(*CHUNKS[-1])
 
     v_two = jnp.concatenate([pad, lower_only(a_ref[...], 64)], axis=0).T
     high, low = split2(v_two)
@@ -407,7 +402,7 @@
         return 0
 
     lax.fori_loop(0, ROWS // BIG, round_three, 0)
-    second_of(ROWS // BIG * BIG, ROWS % BIG, ROWS // BIG, ROWS // BIG * BIG // 128)
+    second_of(*CHUNKS[-1], len(CHUNKS) - 1, CHUNKS[-1][0] // 128)
 
     entry = lax.broadcasted_iota(jnp.int32, (38, 128), 0) * 128 + lax.broadcasted_iota(jnp.int32, (38, 128), 1)
     live = jnp.where(entry < alive, 1.0, 0.0)
@@ -416,9 +411,8 @@
     top_diag = jnp.max(live * diag_ref[...])
     spot = lax.broadcasted_iota(jnp.int32, (1, 128), 1)
     top_ref[...] = jnp.where(spot < 64, top_left, top_diag)
-    for n in range(ROWS // BIG):
-        send(n * BIG, BIG, n).wait()
-    send(ROWS // BIG * BIG, ROWS % BIG, ROWS // BIG).wait()
+    for n, (start, count) in enumerate(CHUNKS):
+        send(start, count, n).wait()
 
 
 def panels(everybody, pivots, live_blocks, diag, chol_done, new_cols):
@@ -427,69 +421,66 @@
     return pl.pallas_call(
         panel_kernel,
         out_shape=(jax.ShapeDtypeStruct((ROWS, COLS), F32), jax.ShapeDtypeStruct((1, 128), F32)),
-        in_specs=[vmem, vmem, pl.BlockSpec(memory_space=pltpu.SMEM), vmem, hbm, hbm],
+        in_specs=[vmem, vmem, pl.BlockSpec(memory_space=pltpu.SMEM), vmem, vmem, vmem],
         out_specs=(hbm, vmem),
         scratch_shapes=[
-            pltpu.VMEM((ROWS, K), F32),
             pltpu.VMEM((ROWS, COLS), F32),
             pltpu.VMEM((ROWS, 128), F32),
             pltpu.VMEM((COLS, K), F32),
             pltpu.VMEM((K, COLS), F32),
-            pltpu.VMEM((K, COLS), BF16),
-            pltpu.VMEM((K, COLS), BF16),
+            pltpu.VMEM((K, 2 * COLS), BF16),
             pltpu.VMEM((2, ORDER, COLS), F32),
             pltpu.VMEM((ORDER, 256), F32),
             pltpu.VMEM((256, 256), BF16),
             pltpu.VMEM((256, 256), BF16),
-            pltpu.VMEM((256, 512), BF16),
-            pltpu.VMEM((256, 512), BF16),
+            pltpu.VMEM((256, 1024), BF16),
             pltpu.VMEM((38, 128), F32),
-            pltpu.SemaphoreType.DMA((2, ROUNDS + 1)),
-            pltpu.SemaphoreType.DMA((ROUNDS + 1,)),
+            pltpu.SemaphoreType.DMA((len(CHUNKS),)),
         ],
         compiler_params=pltpu.CompilerParams(vmem_limit_bytes=VMEM_LIMIT),
     )(everybody, pivots, live_blocks, diag, chol_done, new_cols)
 
 
-def top_kernel(in_ref, out_ref, table, own_sem, near_send, near_recv, far_send, far_recv):
+def top_kernel(in_ref, out_ref, table, own_sem, send_sem, recv_sem):
     grp, blk = lax.axis_index("grp"), lax.axis_index("blk")
+    x, y = lax.div(blk, 4), lax.rem(blk, 4)
+    peers = (
+        [(lax.rem(grp + k, 8), blk) for k in range(1, 8)],
+        [(grp, lax.rem(x + k, 4) * 4 + y) for k in range(1, 4)],
+        [(grp, x * 4 + lax.rem(y + k, 4)) for k in range(1, 4)],
+    )
     barrier = pltpu.get_barrier_semaphore()
-    near = [(lax.rem(grp + k, 8), blk) for k in range(1, 8)]
-    far = [(grp, lax.rem(blk + k, 16)) for k in range(1, 16)]
-    for there in near + far:
-        pl.semaphore_signal(barrier, inc=1, device_id=there, device_id_type=MESH)
-    mine = table.at[blk, grp]
+    for group in peers:
+        for there in group:
+            pl.semaphore_signal(barrier, inc=1, device_id=there, device_id_type=MESH)
+    mine = table.at[x, y, grp]
     own = pltpu.make_async_copy(in_ref, mine, own_sem)
     own.start()
-    pl.semaphore_wait(barrier, len(near) + len(far))
-    one = []
-    for n, there in enumerate(near):
-        copy = pltpu.make_async_remote_copy(
-            src_ref=in_ref, dst_ref=mine, send_sem=near_send.at[n], recv_sem=near_recv.at[n],
-            device_id=there, device_id_type=MESH,
-        )
-        copy.start()
-        one.append(copy)
-    own.wait()
-    for copy in one:
-        copy.wait_recv()
-    two = []
-    for n, there in enumerate(far):
-        copy = pltpu.make_async_remote_copy(
-            src_ref=table.at[blk], dst_ref=table.at[blk], send_sem=far_send.at[n], recv_sem=far_recv.at[n],
-            device_id=there, device_id_type=MESH,
-        )
-        copy.start()
-        two.append(copy)
-    for copy in two:
-        copy.wait_recv()
+    pl.semaphore_wait(barrier, 13)
+    sent = []
+    for phase, (source, target) in enumerate(
+        ((in_ref, mine), (table.at[x, y], table.at[x, y]), (table.at[:, y], table.at[:, y]))
+    ):
+        if phase == 1:
+            own.wait()
+        flying = []
+        for n, there in enumerate(peers[phase]):
+            copy = pltpu.make_async_remote_copy(
+                src_ref=source, dst_ref=target, send_sem=send_sem.at[phase, n], recv_sem=recv_sem.at[phase, n],
+                device_id=there, device_id_type=MESH,
+            )
+            copy.start()
+            flying.append(copy)
+        for copy in flying:
+            copy.wait_recv()
+        sent += flying
     best = jnp.max(table[...].reshape(128, 128), axis=0, keepdims=True)
     spot = lax.broadcasted_iota(jnp.int32, (1, 128), 1)
     low = -3.0e38
     left = jnp.max(jnp.where(spot < 64, best, low), axis=1, keepdims=True)
     diag = jnp.max(jnp.where(spot < 64, low, best), axis=1, keepdims=True)
     out_ref[...] = jnp.broadcast_to(left / diag, (1, 128))
-    for copy in one + two:
+    for copy in sent:
         copy.wait_send()
 
 
@@ -500,14 +491,12 @@
         in_specs=[pl.BlockSpec(memory_space=pltpu.VMEM)],
         out_specs=pl.BlockSpec(memory_space=pltpu.VMEM),
         scratch_shapes=[
-            pltpu.VMEM((16, 8, 1, 128), F32),
+            pltpu.VMEM((4, 4, 8, 1, 128), F32),
             pltpu.SemaphoreType.DMA,
-            pltpu.SemaphoreType.DMA((7,)),
-            pltpu.SemaphoreType.DMA((7,)),
-            pltpu.SemaphoreType.DMA((15,)),
-            pltpu.SemaphoreType.DMA((15,)),
+            pltpu.SemaphoreType.DMA((3, 7)),
+            pltpu.SemaphoreType.DMA((3, 7)),
         ],
-        compiler_params=pltpu.CompilerParams(collective_id=1, has_side_effects=True),
+        compiler_params=pltpu.CompilerParams(collective_id=1, has_side_effects=True, vmem_limit_bytes=2 * 1024 * 1024),
     )(mine)
 
 

time: 71.7 us -> 66.5 us (0.927)
  Pallas kernels: 68.9 us -> 63.5 us
  local copies, waits for them, and re-layouts: 0 us -> 0.76 us
    pallas_call x1, Pallas kernels: 28.6 us -> 24.4 us  [panels(): pl.pallas_call(panel_kernel, out_shape=(jax.ShapeDtypeStruct((ROWS, COLS)...]
    pallas_call x1, Pallas kernels: 25 us -> 22.7 us  [gather(): pl.pallas_call(gather_kernel, out_shape=jax.ShapeDtypeStruct((4, 2, 4, 4,...]
    pallas_call x1, Pallas kernels: 12.8 us -> 13.7 us  [top(): pl.pallas_call(top_kernel, out_shape=jax.ShapeDtypeStruct((1, 128), F32),...]
    unnamed x0 -> x16, local copies, waits for them, and re-layouts: none -> 0.76 us
where the time goes in v3:
time: 66.5 us; the launch traced here: 66.2 us
  Pallas kernels  63.5 us (95%)
  between operations  1.92 us (3%)
  local copies, waits for them, and re-layouts  0.76 us (1%)
    pallas_call x1, Pallas kernels, panels(): pl.pallas_call(panel_kernel, out_shape=(jax.ShapeDtypeStruct((ROWS, COLS)...  24.4 us
    pallas_call x1, Pallas kernels, gather(): pl.pallas_call(gather_kernel, out_shape=jax.ShapeDtypeStruct((4, 2, 4, 4,...  22.7 us
    pallas_call x1, Pallas kernels, top(): pl.pallas_call(top_kernel, out_shape=jax.ShapeDtypeStruct((1, 128), F32),...  13.7 us
    pallas_call x1, Pallas kernels, pick(): pl.pallas_call(pick_kernel, out_shape=jax.ShapeDtypeStruct((SLOT_ROWS, 12...  2.7 us

profile of v3, /device:TPU:0, one launch (start us, length us, event | category | flops | bytes accessed | tf_op | source)
XLA Modules:
  0.0 66.2 jit_solution(9395703411468907042)
XLA Ops:
  0.6 0.0 slice-start
  0.6 2.7 %shard_map.68.in_ref = f32[40,128]{1,0:T(8,128)} custom-call(s32[2,192]{1,0:T(2,128)} %piv_ref.3, f32[4864,512]{1,0:T(8,128)} %chol.1, f32[4864,384]{1,0:T(8,128)} %cols.1), custom_call_target="tpu_custom_call" | custom-call | tf_op jit(solution)/shard_map/pallas_call | solution.py:73
  3.3 0.0 copy-start.2
  3.4 0.7 %copy-done.2 = f32[40,128]{1,0:T(8,128)S(1)} copy-done((f32[40,128]{1,0:T(8,128)S(1)}, f32[40,128]{1,0:T(8,128)}, u32[]{:S(2)}) %copy-start.2) | copy-done | bytes 20504
  4.1 0.0 slice-start.1
  4.1 0.0 slice-start.2
  4.1 0.0 copy-start
  4.1 0.0 copy-start.1
  4.1 0.0 copy-start.3
  4.1 0.0 copy-start.4
  4.1 22.7 %shard_map.69 = f32[4,2,4,4,40,128]{5,4,3,2,1,0:T(8,128)S(1)} custom-call(f32[40,128]{1,0:T(8,128)S(1)} %copy-done.2), custom_call_target="tpu_custom_call" | custom-call | flops 20000000000 | bytes 2700000 | tf_op jit(solution)/shard_map/pallas_call | solution.py:179
  26.9 0.0 slice-done
  26.9 0.0 slice-done.1
  26.9 0.0 slice-done.2
  26.9 0.0 copy-done
  26.9 0.0 copy-done.1
  26.9 0.0 copy-done.3
  26.9 0.0 copy-done.4
  26.9 24.4 %shard_map.70 = (f32[4864,384]{1,0:T(8,128)}, f32[1,128]{1,0:T(1,128)S(1)}) custom-call(f32[5120,128]{1,0:T(8,128)S(1)} %bitcast.6, s32[2,192]{1,0:T(2,128)S(1)} %copy-done.3, s32[128]{0:T(128)S(1)} %copy-done.4, f32[38,128]{1,0:T(8,128)S(1)} %bitcast.7, f32[4864,512]{1,0:T(8,128)S(1)} %bitcast.5, f32[4864,384]{1,0:T(8,128)S(1)} %copy-done), custom_call_target="tpu_custom_call" | custom-call | tf_op jit(solution)/shard_map/pallas_call | solution.py:421
  51.3 13.7 %shard_map.71 = f32[1,128]{1,0:T(1,128)S(1)} custom-call(f32[1,128]{1,0:T(1,128)S(1)} %get-tuple-element.5.in_ref), custom_call_target="tpu_custom_call" | custom-call | tf_op jit(solution)/shard_map/pallas_call | solution.py:488
  (1 shorter events, 0.0 us)
Async XLA Ops:
  0.6 26.2 %slice-start = ((s8[9961472]{0:T(1024)(128)(4,1)}), s8[1572864]{0:T(1024)(128)(4,1)S(1)}, s32[]{:S(2)}) async-start(s8[9961472]{0:T(1024)(128)(4,1)} %bitcast.4), calls=%async_computation | async-start | bytes 3145728
  3.3 0.7 %copy-start.2 = (f32[40,128]{1,0:T(8,128)S(1)}, f32[40,128]{1,0:T(8,128)}, u32[]{:S(2)}) copy-start(f32[40,128]{1,0:T(8,128)} %shard_map.68.in_ref) | copy-start | bytes 61444
  4.1 22.8 %slice-start.1 = ((s8[9961472]{0:T(1024)(128)(4,1)}), s8[4194304]{0:T(1024)(128)(4,1)S(1)}, s32[]{:S(2)}) async-start(s8[9961472]{0:T(1024)(128)(4,1)} %bitcast.4), calls=%async_computation.1 | async-start | bytes 8388608
  4.1 22.8 %slice-start.2 = ((s8[9961472]{0:T(1024)(128)(4,1)}), s8[4194304]{0:T(1024)(128)(4,1)S(1)}, s32[]{:S(2)}) async-start(s8[9961472]{0:T(1024)(128)(4,1)} %bitcast.4), calls=%async_computation.2 | async-start | bytes 8388608
  4.1 22.8 %copy-start = (f32[4864,384]{1,0:T(8,128)S(1)}, f32[4864,384]{1,0:T(8,128)}, u32[]{:S(2)}) copy-start(f32[4864,384]{1,0:T(8,128)} %cols.1) | copy-start | bytes 22413316
  4.1 22.8 %copy-start.1 = (f32[4864]{0:T(1024)S(1)}, f32[4864]{0:T(1024)}, u32[]{:S(2)}) copy-start(f32[4864]{0:T(1024)} %param.7) | copy-start | bytes 58372
  4.1 22.8 %copy-start.3 = (s32[2,192]{1,0:T(2,128)S(1)}, s32[2,192]{1,0:T(2,128)}, u32[]{:S(2)}) copy-start(s32[2,192]{1,0:T(2,128)} %piv_ref.3) | copy-start | bytes 4612
  4.1 22.8 %copy-start.4 = (s32[128]{0:T(128)S(1)}, s32[128]{0:T(128)}, u32[]{:S(2)}) copy-start(s32[128]{0:T(128)} %live_ref.1) | copy-start | bytes 1540

commit v4 on v3

--- a/solution.py
+++ b/solution.py
@@ -6,7 +6,6 @@
 from jax.sharding import PartitionSpec as P
 
 MESH = pl.DeviceIdType.MESH
-HIGHEST = lax.Precision.HIGHEST
 F32 = jnp.float32
 BF16 = jnp.bfloat16
 ROWS = 4864
@@ -84,7 +83,7 @@
             pltpu.VMEM((6, 8, COLS), F32),
             pltpu.SemaphoreType.DMA((2, 6)),
         ],
-        compiler_params=pltpu.CompilerParams(vmem_limit_bytes=60 * 1024 * 1024),
+        compiler_params=pltpu.CompilerParams(vmem_limit_bytes=50 * 1024 * 1024),
     )(pivots, chol_done, new_cols)
 
 
@@ -212,10 +211,6 @@
 def mul3(a, b_high, b_low):
     high, low = split2(a)
     return mul(high, b_high) + (mul(high, b_low) + mul(low, b_high))
-
-
-def exact(a, b):
-    return jnp.dot(a, b, precision=HIGHEST, preferred_element_type=F32)
 
 
 def over_lanes(x, lane):
@@ -285,7 +280,7 @@
 
 
 def panel_kernel(g_ref, piv_ref, live_ref, diag_ref, chol, cols, out_hbm, top_ref,
-                 rbuf, squares, hmat, htr, ht_pair, head, a_ref,
+                 rbuf, squares, hmat, ht_pair, head, a_ref,
                  v_high, v_low, w_pair, sums, out_sem):
     me = lax.axis_index("grp") * 16 + lax.axis_index("blk")
     alive = live_ref[me] * BLOCK_ROWS
@@ -302,22 +297,27 @@
         hot = jnp.concatenate(
             [jnp.where((dev == owner) & (rank == float(s)), 1.0, 0.0) for s in range(SLOTS)], axis=1
         ).astype(BF16)
-        for c in range(6 if panel == 0 else 7):
+        def chunk(c):
             pieces = [g_ref[pl.ds(slot_base(panel, s) + c, 128, stride=SLOT_ROWS), :] for s in range(SLOTS)]
-            high, mid, low = split3(jnp.concatenate(pieces, axis=0))
-            rows = mul(hot, high) + (mul(hot, mid) + mul(hot, low))
-            if c < 4:
-                hmat[panel * ORDER : (panel + 1) * ORDER, c * 128 : (c + 1) * 128] = rows
-            else:
-                head[panel, :, (c - 4) * 128 : (c - 3) * 128] = rows
-    htr[...] = hmat[...].T
-    lanes = lax.broadcasted_iota(jnp.int32, (ORDER, 256), 1)
-    one = head[0, :, 0:256] - exact(hmat[0:ORDER, :], htr[:, 0:256])
-    a_ref[...] = jnp.where(lanes < ORDER, one, 0.0)
-    head[1, :, :] = head[1, :, :] - exact(hmat[ORDER:, :], htr[...])
-    high, low = split2(htr[...])
+            return jnp.concatenate(pieces, axis=0)
+
+        mine = pl.ds(panel * ORDER, ORDER)
+        for c in (0, 2):
+            high, low = split2(jnp.concatenate([chunk(c), chunk(c + 1)], axis=1))
+            hmat[mine, c * 128 : (c + 2) * 128] = mul(hot, high) + mul(hot, low)
+        high, mid, low = split3(jnp.concatenate([chunk(4), chunk(5)], axis=1))
+        head[panel, :, 0:256] = mul(hot, high) + (mul(hot, mid) + mul(hot, low))
+        if panel == 1:
+            high, mid, low = split3(chunk(6))
+            head[panel, :, 256:384] = mul(hot, high) + (mul(hot, mid) + mul(hot, low))
+    high, low = split2(hmat[...].T)
     ht_pair[:, 0:COLS] = high
     ht_pair[:, COLS:] = low
+
+    lanes = lax.broadcasted_iota(jnp.int32, (ORDER, 256), 1)
+    known = mul3(hmat[...], ht_pair[:, 0:COLS], ht_pair[:, COLS:])
+    a_ref[...] = jnp.where(lanes < ORDER, head[0, :, 0:256] - known[0:ORDER, 0:256], 0.0)
+    head[1, :, :] = head[1, :, :] - known[ORDER:, :]
 
     def residual_high(start, count):
         rows = pl.ds(start, count)
@@ -347,13 +347,17 @@
 
     pad = jnp.zeros((64, 256), F32)
     v_one = jnp.concatenate([lower_only(a_ref[...], 0), pad], axis=0).T
-    f_rows = exact(head[1, :, 0:256], v_one)
+    high, low = split2(v_one)
+    w_pair[:, 0:256] = high
+    w_pair[:, 512:768] = low
+    f_rows = mul3(head[1, :, 0:256], high, low)
     f_tr = jnp.concatenate([pad, f_rows], axis=0).T
-    two = head[1, :, 128:384] - exact(f_rows, f_tr)
+    high, low = split2(f_tr)
+    two = head[1, :, 128:384] - mul3(f_rows, high, low)
     a_ref[...] = jnp.where(lanes >= 64, two, 0.0)
-    high, low = split2(jnp.concatenate([v_one, exact(v_one, f_tr)], axis=1))
-    w_pair[:, 0:512] = high
-    w_pair[:, 512:] = low
+    high, low = split2(mul3(v_one, high, low))
+    w_pair[:, 256:512] = high
+    w_pair[:, 768:] = low
 
     def first_of(start, count):
         rows = pl.ds(start, count)
@@ -427,7 +431,6 @@
             pltpu.VMEM((ROWS, COLS), F32),
             pltpu.VMEM((ROWS, 128), F32),
             pltpu.VMEM((COLS, K), F32),
-            pltpu.VMEM((K, COLS), F32),
             pltpu.VMEM((K, 2 * COLS), BF16),
             pltpu.VMEM((2, ORDER, COLS), F32),
             pltpu.VMEM((ORDER, 256), F32),

time: 66.5 us -> 63.6 us (0.956)
  Pallas kernels: 63.5 us -> 60.8 us
    pallas_call x1, Pallas kernels: 24.4 us -> 23 us  [panels(): pl.pallas_call(panel_kernel, out_shape=(jax.ShapeDtypeStruct((ROWS, COLS)...]
    pallas_call x1, Pallas kernels: 2.7 us -> 1.4 us  [pick(): pl.pallas_call(pick_kernel, out_shape=jax.ShapeDtypeStruct((SLOT_ROWS, 12...]
where the time goes in v4:
time: 63.6 us; the launch traced here: 63.5 us
  Pallas kernels  60.8 us (96%)
  between operations  1.95 us (3%)
  local copies, waits for them, and re-layouts  0.72 us (1%)
    pallas_call x1, Pallas kernels, panels(): pl.pallas_call(panel_kernel, out_shape=(jax.ShapeDtypeStruct((ROWS, COLS)...  23 us
    pallas_call x1, Pallas kernels, gather(): pl.pallas_call(gather_kernel, out_shape=jax.ShapeDtypeStruct((4, 2, 4, 4,...  22.8 us
    pallas_call x1, Pallas kernels, top(): pl.pallas_call(top_kernel, out_shape=jax.ShapeDtypeStruct((1, 128), F32),...  13.6 us
    pallas_call x1, Pallas kernels, pick(): pl.pallas_call(pick_kernel, out_shape=jax.ShapeDtypeStruct((SLOT_ROWS, 12...  1.4 us

profile of v4, /device:TPU:0, one launch (start us, length us, event | category | flops | bytes accessed | tf_op | source)
XLA Modules:
  0.0 63.5 jit_solution(18246352311521517983)
XLA Ops:
  0.6 0.0 copy-start.1
  0.6 0.7 %copy-done.1 = s32[2,192]{1,0:T(2,128)S(1)} copy-done((s32[2,192]{1,0:T(2,128)S(1)}, s32[2,192]{1,0:T(2,128)}, u32[]{:S(2)}) %copy-start.1) | copy-done | bytes 1560
  1.3 0.0 slice-start
  1.3 0.0 slice-start.3
  1.3 1.4 %shard_map.68.in_ref = f32[40,128]{1,0:T(8,128)S(1)} custom-call(s32[2,192]{1,0:T(2,128)S(1)} %copy-done.1, f32[4864,512]{1,0:T(8,128)} %chol.1, f32[4864,384]{1,0:T(8,128)} %cols.1), custom_call_target="tpu_custom_call" | custom-call | tf_op jit(solution)/shard_map/pallas_call | solution.py:72
  2.7 0.0 slice-start.1
  2.7 0.0 slice-start.2
  2.8 0.0 slice-start.4
  2.8 0.0 copy-start
  2.8 0.0 copy-start.2
  2.8 0.0 copy-start.3
  2.8 22.8 %shard_map.69 = f32[4,2,4,4,40,128]{5,4,3,2,1,0:T(8,128)S(1)} custom-call(f32[40,128]{1,0:T(8,128)S(1)} %shard_map.68.in_ref), custom_call_target="tpu_custom_call" | custom-call | flops 20000000000 | bytes 2700000 | tf_op jit(solution)/shard_map/pallas_call | solution.py:178
  25.6 0.0 slice-done
  25.6 0.0 slice-done.3
  25.6 0.0 slice-done.1
  25.6 0.0 slice-done.2
  25.6 0.0 slice-done.4
  25.6 0.0 copy-done
  25.7 0.0 copy-done.2
  25.7 0.0 copy-done.3
  25.7 23.0 %shard_map.70 = (f32[4864,384]{1,0:T(8,128)}, f32[1,128]{1,0:T(1,128)S(1)}) custom-call(f32[5120,128]{1,0:T(8,128)S(1)} %bitcast.8, s32[2,192]{1,0:T(2,128)S(1)} %copy-done.2, s32[128]{0:T(128)S(1)} %copy-done.3, f32[38,128]{1,0:T(8,128)S(1)} %bitcast.9, f32[4864,512]{1,0:T(8,128)S(1)} %bitcast.5, f32[4864,384]{1,0:T(8,128)S(1)} %bitcast.7), custom_call_target="tpu_custom_call" | custom-call | tf_op jit(solution)/shard_map/pallas_call | solution.py:425
  48.7 13.6 %shard_map.71 = f32[1,128]{1,0:T(1,128)S(1)} custom-call(f32[1,128]{1,0:T(1,128)S(1)} %get-tuple-element.5.in_ref), custom_call_target="tpu_custom_call" | custom-call | tf_op jit(solution)/shard_map/pallas_call | solution.py:491
  (2 shorter events, 0.0 us)
Async XLA Ops:
  0.6 0.7 %copy-start.1 = (s32[2,192]{1,0:T(2,128)S(1)}, s32[2,192]{1,0:T(2,128)}, u32[]{:S(2)}) copy-start(s32[2,192]{1,0:T(2,128)} %piv_ref.3) | copy-start | bytes 4612
  1.3 24.3 %slice-start = ((s8[9961472]{0:T(1024)(128)(4,1)}), s8[1572864]{0:T(1024)(128)(4,1)S(1)}, s32[]{:S(2)}) async-start(s8[9961472]{0:T(1024)(128)(4,1)} %bitcast.4), calls=%async_computation | async-start | bytes 3145728
  1.3 24.3 %slice-start.3 = ((s8[7471104]{0:T(1024)(128)(4,1)}), s8[4194304]{0:T(1024)(128)(4,1)S(1)}, s32[]{:S(2)}) async-start(s8[7471104]{0:T(1024)(128)(4,1)} %bitcast.6), calls=%async_computation.3 | async-start | bytes 8388608
  2.7 22.9 %slice-start.1 = ((s8[9961472]{0:T(1024)(128)(4,1)}), s8[4194304]{0:T(1024)(128)(4,1)S(1)}, s32[]{:S(2)}) async-start(s8[9961472]{0:T(1024)(128)(4,1)} %bitcast.4), calls=%async_computation.1 | async-start | bytes 8388608
  2.7 22.9 %slice-start.2 = ((s8[9961472]{0:T(1024)(128)(4,1)}), s8[4194304]{0:T(1024)(128)(4,1)S(1)}, s32[]{:S(2)}) async-start(s8[9961472]{0:T(1024)(128)(4,1)} %bitcast.4), calls=%async_computation.2 | async-start | bytes 8388608
  2.8 22.9 %slice-start.4 = ((s8[7471104]{0:T(1024)(128)(4,1)}), s8[3276800]{0:T(1024)(128)(4,1)S(1)}, s32[]{:S(2)}) async-start(s8[7471104]{0:T(1024)(128)(4,1)} %bitcast.6), calls=%async_computation.4 | async-start | bytes 6553600
  2.8 22.9 %copy-start = (f32[4864]{0:T(1024)S(1)}, f32[4864]{0:T(1024)}, u32[]{:S(2)}) copy-start(f32[4864]{0:T(1024)} %param.7) | copy-start | bytes 58372
  2.8 22.9 %copy-start.2 = (s32[2,192]{1,0:T(2,128)S(1)}, s32[2,192]{1,0:T(2,128)}, u32[]{:S(2)}) copy-start(s32[2,192]{1,0:T(2,128)} %piv_ref.3) | copy-start | bytes 4612
  2.8 22.9 %copy-start.3 = (s32[128]{0:T(128)S(1)}, s32[128]{0:T(128)}, u32[]{:S(2)}) copy-start(s32[128]{0:T(128)} %live_ref.1) | copy-start | bytes 1540

commit v5 on v4

--- a/solution.py
+++ b/solution.py
@@ -21,7 +21,7 @@
 TILE = 384
 CHUNKS = [(i * BIG, BIG) for i in range(ROWS // BIG)] + [(ROWS // BIG * BIG, ROWS % BIG)]
 VMEM_LIMIT = 24 * 1024 * 1024
-COLOURS = ((0, 16, "yxz"), (16, 16, "xzy"), (32, 8, "zyx"))
+COLOURS = ((0, 13, "yxz"), (13, 13, "xzy"), (26, 13, "zyx"))
 
 
 def slot_base(panel, slot):
@@ -221,7 +221,7 @@
     return jnp.broadcast_to(x[row : row + 1, :], (8, 128))
 
 
-def factor_round(a_ref, r, off):
+def factor_round(a_ref, left_ref, right_ref, r, off):
     rs = pl.multiple_of(r * STEP, STEP)
     c0 = off + r * STEP
     t = c0 // 128
@@ -261,15 +261,17 @@
     u = jnp.concatenate([jnp.concatenate([row[q, h] for h in range(2)], axis=1) for q in range(2)], axis=0)
     lanes = lax.broadcasted_iota(jnp.int32, (STEP, 256), 1)
     high, mid, low3 = split3(u)
-    zero = jnp.zeros_like(u)
-    ahead = lanes >= c0 + STEP
-    h_l, m_l, l_l = split3(jnp.where(ahead, u, zero))
-    left = jnp.concatenate([h_l, h_l, m_l, m_l, h_l, l_l], axis=0)
-    right = jnp.concatenate([high, mid, high, mid, low3, high], axis=0)
-    z = lax.dot_general(left, right, (((0,), (0,)), ((), ())), preferred_element_type=F32)
+    h_l, m_l, l_l = split3(jnp.where(lanes >= c0 + STEP, u, 0.0))
+    left_ref[...] = jnp.concatenate([h_l, h_l, m_l, m_l, h_l, l_l], axis=0)
+    right_ref[...] = jnp.concatenate([high, mid, high, mid, low3, high], axis=0)
+
+
+def factor_update(a_ref, left_ref, right_ref, r, off):
+    c0 = off + r * STEP
+    z = lax.dot_general(left_ref[...], right_ref[...], (((0,), (0,)), ((), ())), preferred_element_type=F32)
     rows_i = lax.broadcasted_iota(jnp.int32, (ORDER, 256), 0)
     cols_i = lax.broadcasted_iota(jnp.int32, (ORDER, 256), 1)
-    old = (rows_i >= rs + STEP) & (cols_i >= c0) & (cols_i < c0 + STEP)
+    old = (rows_i >= (r + 1) * STEP) & (cols_i >= c0) & (cols_i < c0 + STEP)
     a_ref[...] = jnp.where(old, 0.0, a_ref[...]) - z[off : off + ORDER, :]
 
 
@@ -280,7 +282,7 @@
 
 
 def panel_kernel(g_ref, piv_ref, live_ref, diag_ref, chol, cols, out_hbm, top_ref,
-                 rbuf, squares, hmat, ht_pair, head, a_ref,
+                 rbuf, squares, hmat, ht_pair, head, a_ref, left_ref, right_ref,
                  v_high, v_low, w_pair, sums, out_sem):
     me = lax.axis_index("grp") * 16 + lax.axis_index("blk")
     alive = live_ref[me] * BLOCK_ROWS
@@ -335,12 +337,17 @@
 
     def round_one(r, _):
         start = pl.multiple_of(r * BIG, BIG)
+        factor_update(a_ref, left_ref, right_ref, 2 * r - 1, 0)
         residual_high(start, BIG)
-        factor_round(a_ref, 2 * r, 0)
+        factor_round(a_ref, left_ref, right_ref, 2 * r, 0)
+        factor_update(a_ref, left_ref, right_ref, 2 * r, 0)
         residual_low(start, BIG)
-        factor_round(a_ref, 2 * r + 1, 0)
+        factor_round(a_ref, left_ref, right_ref, 2 * r + 1, 0)
         return 0
 
+    nothing = jnp.zeros((6 * STEP, 256), BF16)
+    left_ref[...] = nothing
+    right_ref[...] = nothing
     lax.fori_loop(0, ROUNDS // 2, round_one, 0)
     residual_high(*CHUNKS[-1])
     residual_low(*CHUNKS[-1])
@@ -373,10 +380,13 @@
         squares[rows, :] = squares[rows, :] + (first[:, 0:128] * first[:, 0:128] + first[:, 128:256] * first[:, 128:256])
 
     def round_two(r, _):
+        factor_update(a_ref, left_ref, right_ref, r - 1, 64)
         first_of(pl.multiple_of(r * TILE, TILE), TILE)
-        factor_round(a_ref, r, 64)
+        factor_round(a_ref, left_ref, right_ref, r, 64)
         return 0
 
+    left_ref[...] = nothing
+    right_ref[...] = nothing
     lax.fori_loop(0, ROUNDS, round_two, 0)
     first_of(*CHUNKS[-1])
 
@@ -434,6 +444,8 @@
             pltpu.VMEM((K, 2 * COLS), BF16),
             pltpu.VMEM((2, ORDER, COLS), F32),
             pltpu.VMEM((ORDER, 256), F32),
+            pltpu.VMEM((6 * STEP, 256), BF16),
+            pltpu.VMEM((6 * STEP, 256), BF16),
             pltpu.VMEM((256, 256), BF16),
             pltpu.VMEM((256, 256), BF16),
             pltpu.VMEM((256, 1024), BF16),

time: 63.6 us -> 62.4 us (0.981)
  Pallas kernels: 60.8 us -> 59.5 us
    pallas_call x1, Pallas kernels: 22.8 us -> 22.1 us  [gather(): pl.pallas_call(gather_kernel, out_shape=jax.ShapeDtypeStruct((4, 2, 4, 4,...]
where the time goes in v5:
time: 62.4 us; the launch traced here: 62.2 us
  Pallas kernels  59.5 us (95%)
  between operations  1.95 us (3%)
  local copies, waits for them, and re-layouts  0.72 us (1%)
    pallas_call x1, Pallas kernels, panels(): pl.pallas_call(panel_kernel, out_shape=(jax.ShapeDtypeStruct((ROWS, COLS)...  22.6 us
    pallas_call x1, Pallas kernels, gather(): pl.pallas_call(gather_kernel, out_shape=jax.ShapeDtypeStruct((4, 2, 4, 4,...  22.1 us
    pallas_call x1, Pallas kernels, top(): pl.pallas_call(top_kernel, out_shape=jax.ShapeDtypeStruct((1, 128), F32),...  13.4 us
    pallas_call x1, Pallas kernels, pick(): pl.pallas_call(pick_kernel, out_shape=jax.ShapeDtypeStruct((SLOT_ROWS, 12...  1.4 us

profile of v5, /device:TPU:0, one launch (start us, length us, event | category | flops | bytes accessed | tf_op | source)
XLA Modules:
  0.0 62.2 jit_solution(4462538446755336264)
XLA Ops:
  0.6 0.0 copy-start.1
  0.6 0.7 %copy-done.1 = s32[2,192]{1,0:T(2,128)S(1)} copy-done((s32[2,192]{1,0:T(2,128)S(1)}, s32[2,192]{1,0:T(2,128)}, u32[]{:S(2)}) %copy-start.1) | copy-done | bytes 1560
  1.3 0.0 slice-start
  1.3 0.0 slice-start.3
  1.3 1.4 %shard_map.68.in_ref = f32[40,128]{1,0:T(8,128)S(1)} custom-call(s32[2,192]{1,0:T(2,128)S(1)} %copy-done.1, f32[4864,512]{1,0:T(8,128)} %chol.1, f32[4864,384]{1,0:T(8,128)} %cols.1), custom_call_target="tpu_custom_call" | custom-call | tf_op jit(solution)/shard_map/pallas_call | solution.py:72
  2.7 0.0 slice-start.1
  2.7 0.0 slice-start.2
  2.8 0.0 slice-start.4
  2.8 0.0 copy-start
  2.8 0.0 copy-start.2
  2.8 0.0 copy-start.3
  2.8 22.1 %shard_map.69 = f32[4,2,4,4,40,128]{5,4,3,2,1,0:T(8,128)S(1)} custom-call(f32[40,128]{1,0:T(8,128)S(1)} %shard_map.68.in_ref), custom_call_target="tpu_custom_call" | custom-call | flops 20000000000 | bytes 2700000 | tf_op jit(solution)/shard_map/pallas_call | solution.py:178
  24.9 0.0 slice-done
  24.9 0.0 slice-done.3
  24.9 0.0 slice-done.1
  24.9 0.0 slice-done.2
  24.9 0.0 slice-done.4
  24.9 0.0 copy-done
  24.9 0.0 copy-done.2
  24.9 0.0 copy-done.3
  25.0 22.6 %shard_map.70 = (f32[4864,384]{1,0:T(8,128)}, f32[1,128]{1,0:T(1,128)S(1)}) custom-call(f32[5120,128]{1,0:T(8,128)S(1)} %bitcast.8, s32[2,192]{1,0:T(2,128)S(1)} %copy-done.2, s32[128]{0:T(128)S(1)} %copy-done.3, f32[38,128]{1,0:T(8,128)S(1)} %bitcast.9, f32[4864,512]{1,0:T(8,128)S(1)} %bitcast.5, f32[4864,384]{1,0:T(8,128)S(1)} %bitcast.7), custom_call_target="tpu_custom_call" | custom-call | tf_op jit(solution)/shard_map/pallas_call | solution.py:435
  47.6 13.4 %shard_map.71 = f32[1,128]{1,0:T(1,128)S(1)} custom-call(f32[1,128]{1,0:T(1,128)S(1)} %get-tuple-element.5.in_ref), custom_call_target="tpu_custom_call" | custom-call | tf_op jit(solution)/shard_map/pallas_call | solution.py:503
  (2 shorter events, 0.0 us)
Async XLA Ops:
  0.6 0.7 %copy-start.1 = (s32[2,192]{1,0:T(2,128)S(1)}, s32[2,192]{1,0:T(2,128)}, u32[]{:S(2)}) copy-start(s32[2,192]{1,0:T(2,128)} %piv_ref.3) | copy-start | bytes 4612
  1.3 23.6 %slice-start = ((s8[9961472]{0:T(1024)(128)(4,1)}), s8[1572864]{0:T(1024)(128)(4,1)S(1)}, s32[]{:S(2)}) async-start(s8[9961472]{0:T(1024)(128)(4,1)} %bitcast.4), calls=%async_computation | async-start | bytes 3145728
  1.3 23.6 %slice-start.3 = ((s8[7471104]{0:T(1024)(128)(4,1)}), s8[4194304]{0:T(1024)(128)(4,1)S(1)}, s32[]{:S(2)}) async-start(s8[7471104]{0:T(1024)(128)(4,1)} %bitcast.6), calls=%async_computation.3 | async-start | bytes 8388608
  2.7 22.2 %slice-start.1 = ((s8[9961472]{0:T(1024)(128)(4,1)}), s8[4194304]{0:T(1024)(128)(4,1)S(1)}, s32[]{:S(2)}) async-start(s8[9961472]{0:T(1024)(128)(4,1)} %bitcast.4), calls=%async_computation.1 | async-start | bytes 8388608
  2.7 22.2 %slice-start.2 = ((s8[9961472]{0:T(1024)(128)(4,1)}), s8[4194304]{0:T(1024)(128)(4,1)S(1)}, s32[]{:S(2)}) async-start(s8[9961472]{0:T(1024)(128)(4,1)} %bitcast.4), calls=%async_computation.2 | async-start | bytes 8388608
  2.8 22.2 %slice-start.4 = ((s8[7471104]{0:T(1024)(128)(4,1)}), s8[3276800]{0:T(1024)(128)(4,1)S(1)}, s32[]{:S(2)}) async-start(s8[7471104]{0:T(1024)(128)(4,1)} %bitcast.6), calls=%async_computation.4 | async-start | bytes 6553600
  2.8 22.2 %copy-start = (f32[4864]{0:T(1024)S(1)}, f32[4864]{0:T(1024)}, u32[]{:S(2)}) copy-start(f32[4864]{0:T(1024)} %param.7) | copy-start | bytes 58372
  2.8 22.1 %copy-start.2 = (s32[2,192]{1,0:T(2,128)S(1)}, s32[2,192]{1,0:T(2,128)}, u32[]{:S(2)}) copy-start(s32[2,192]{1,0:T(2,128)} %piv_ref.3) | copy-start | bytes 4612
  2.8 22.1 %copy-start.3 = (s32[128]{0:T(128)S(1)}, s32[128]{0:T(128)}, u32[]{:S(2)}) copy-start(s32[128]{0:T(128)} %live_ref.1) | copy-start | bytes 1540

commit v6 on v5

--- a/solution.py
+++ b/solution.py
@@ -121,7 +121,7 @@
         first, count, order = COLOURS[colour]
         have = order[:phase]
         here = region(colour, have, at)
-        for k in (2, 1, 3):
+        for k in (3, 2, 1):
             source = in_ref.at[pl.ds(first, count), :] if phase == 0 else here
             copy = pltpu.make_async_remote_copy(
                 src_ref=source,
@@ -154,12 +154,12 @@
     own.wait()
     for phase in (1, 2):
         for colour in colours:
-            for k in (1, 3, 2):
+            for k in (3, 2, 1):
                 flights[colour, phase - 1, k].wait_recv()
             launch(colour, phase)
             if phase == 2:
                 hand_over(colour, 0, region(colour, COLOURS[colour][2][:2], at))
-    for k in (1, 3, 2):
+    for k in (3, 2, 1):
         for colour in colours:
             flights[colour, 2, k].wait_recv()
             last = COLOURS[colour][2][2]

time: 62.4 us -> 62.2 us (level)
    pallas_call x1, Pallas kernels: 22.1 us -> 21.1 us  [gather(): pl.pallas_call(gather_kernel, out_shape=jax.ShapeDtypeStruct((4, 2, 4, 4,...]
    pallas_call x1, Pallas kernels: 13.4 us -> 14.2 us  [top(): pl.pallas_call(top_kernel, out_shape=jax.ShapeDtypeStruct((1, 128), F32),...]
where the time goes in v6:
time: 62.2 us; the launch traced here: 62 us
  Pallas kernels  59.3 us (95%)
  between operations  1.95 us (3%)
  local copies, waits for them, and re-layouts  0.72 us (1%)
    pallas_call x1, Pallas kernels, panels(): pl.pallas_call(panel_kernel, out_shape=(jax.ShapeDtypeStruct((ROWS, COLS)...  22.6 us
    pallas_call x1, Pallas kernels, gather(): pl.pallas_call(gather_kernel, out_shape=jax.ShapeDtypeStruct((4, 2, 4, 4,...  21.1 us
    pallas_call x1, Pallas kernels, top(): pl.pallas_call(top_kernel, out_shape=jax.ShapeDtypeStruct((1, 128), F32),...  14.2 us
    pallas_call x1, Pallas kernels, pick(): pl.pallas_call(pick_kernel, out_shape=jax.ShapeDtypeStruct((SLOT_ROWS, 12...  1.4 us

profile of v6, /device:TPU:0, one launch (start us, length us, event | category | flops | bytes accessed | tf_op | source)
XLA Modules:
  0.0 62.0 jit_solution(12274472923003358175)
XLA Ops:
  0.6 0.0 copy-start.1
  0.6 0.7 %copy-done.1 = s32[2,192]{1,0:T(2,128)S(1)} copy-done((s32[2,192]{1,0:T(2,128)S(1)}, s32[2,192]{1,0:T(2,128)}, u32[]{:S(2)}) %copy-start.1) | copy-done | bytes 1560
  1.3 0.0 slice-start
  1.3 0.0 slice-start.3
  1.3 1.4 %shard_map.68.in_ref = f32[40,128]{1,0:T(8,128)S(1)} custom-call(s32[2,192]{1,0:T(2,128)S(1)} %copy-done.1, f32[4864,512]{1,0:T(8,128)} %chol.1, f32[4864,384]{1,0:T(8,128)} %cols.1), custom_call_target="tpu_custom_call" | custom-call | tf_op jit(solution)/shard_map/pallas_call | solution.py:72
  2.7 0.0 slice-start.1
  2.7 0.0 slice-start.2
  2.8 0.0 slice-start.4
  2.8 0.0 copy-start
  2.8 0.0 copy-start.2
  2.8 0.0 copy-start.3
  2.8 21.1 %shard_map.69 = f32[4,2,4,4,40,128]{5,4,3,2,1,0:T(8,128)S(1)} custom-call(f32[40,128]{1,0:T(8,128)S(1)} %shard_map.68.in_ref), custom_call_target="tpu_custom_call" | custom-call | flops 20000000000 | bytes 2700000 | tf_op jit(solution)/shard_map/pallas_call | solution.py:178
  24.0 0.0 slice-done
  24.0 0.0 slice-done.3
  24.0 0.0 slice-done.1
  24.0 0.0 slice-done.2
  24.0 0.0 slice-done.4
  24.0 0.0 copy-done
  24.0 0.0 copy-done.2
  24.0 0.0 copy-done.3
  24.1 22.6 %shard_map.70 = (f32[4864,384]{1,0:T(8,128)}, f32[1,128]{1,0:T(1,128)S(1)}) custom-call(f32[5120,128]{1,0:T(8,128)S(1)} %bitcast.8, s32[2,192]{1,0:T(2,128)S(1)} %copy-done.2, s32[128]{0:T(128)S(1)} %copy-done.3, f32[38,128]{1,0:T(8,128)S(1)} %bitcast.9, f32[4864,512]{1,0:T(8,128)S(1)} %bitcast.5, f32[4864,384]{1,0:T(8,128)S(1)} %bitcast.7), custom_call_target="tpu_custom_call" | custom-call | tf_op jit(solution)/shard_map/pallas_call | solution.py:435
  46.7 14.2 %shard_map.71 = f32[1,128]{1,0:T(1,128)S(1)} custom-call(f32[1,128]{1,0:T(1,128)S(1)} %get-tuple-element.5.in_ref), custom_call_target="tpu_custom_call" | custom-call | tf_op jit(solution)/shard_map/pallas_call | solution.py:503
  (2 shorter events, 0.0 us)
Async XLA Ops:
  0.6 0.7 %copy-start.1 = (s32[2,192]{1,0:T(2,128)S(1)}, s32[2,192]{1,0:T(2,128)}, u32[]{:S(2)}) copy-start(s32[2,192]{1,0:T(2,128)} %piv_ref.3) | copy-start | bytes 4612
  1.3 22.6 %slice-start = ((s8[9961472]{0:T(1024)(128)(4,1)}), s8[1572864]{0:T(1024)(128)(4,1)S(1)}, s32[]{:S(2)}) async-start(s8[9961472]{0:T(1024)(128)(4,1)} %bitcast.4), calls=%async_computation | async-start | bytes 3145728
  1.3 22.7 %slice-start.3 = ((s8[7471104]{0:T(1024)(128)(4,1)}), s8[4194304]{0:T(1024)(128)(4,1)S(1)}, s32[]{:S(2)}) async-start(s8[7471104]{0:T(1024)(128)(4,1)} %bitcast.6), calls=%async_computation.3 | async-start | bytes 8388608
  2.7 21.3 %slice-start.1 = ((s8[9961472]{0:T(1024)(128)(4,1)}), s8[4194304]{0:T(1024)(128)(4,1)S(1)}, s32[]{:S(2)}) async-start(s8[9961472]{0:T(1024)(128)(4,1)} %bitcast.4), calls=%async_computation.1 | async-start | bytes 8388608
  2.7 21.2 %slice-start.2 = ((s8[9961472]{0:T(1024)(128)(4,1)}), s8[4194304]{0:T(1024)(128)(4,1)S(1)}, s32[]{:S(2)}) async-start(s8[9961472]{0:T(1024)(128)(4,1)} %bitcast.4), calls=%async_computation.2 | async-start | bytes 8388608
  2.8 21.2 %slice-start.4 = ((s8[7471104]{0:T(1024)(128)(4,1)}), s8[3276800]{0:T(1024)(128)(4,1)S(1)}, s32[]{:S(2)}) async-start(s8[7471104]{0:T(1024)(128)(4,1)} %bitcast.6), calls=%async_computation.4 | async-start | bytes 6553600
  2.8 21.2 %copy-start = (f32[4864]{0:T(1024)S(1)}, f32[4864]{0:T(1024)}, u32[]{:S(2)}) copy-start(f32[4864]{0:T(1024)} %param.7) | copy-start | bytes 58372
  2.8 21.2 %copy-start.2 = (s32[2,192]{1,0:T(2,128)S(1)}, s32[2,192]{1,0:T(2,128)}, u32[]{:S(2)}) copy-start(s32[2,192]{1,0:T(2,128)} %piv_ref.3) | copy-start | bytes 4612
  2.8 21.2 %copy-start.3 = (s32[128]{0:T(128)S(1)}, s32[128]{0:T(128)}, u32[]{:S(2)}) copy-start(s32[128]{0:T(128)} %live_ref.1) | copy-start | bytes 1540
